TPU v7x, 32 devices: a whole 2x2x4 slice. The times are simulated.
32 devices in a mesh: seq: 16 (over z, y, core), batch: 2 (over x).
Axes of the slice: x: 2, y: 2, z: 4, core: 2. Of those that a mesh axis runs over, the one named last changes fastest.
Arguments:
- tokens: bfloat16 [2, 2, 4096, 1024], P(None, 'batch', 'seq'), may hold values from -6 to 6
- segments: int32 [2, 2, 4096], P(None, 'batch'), may hold values from 0 to 3, never falling along the last dimension, each value on 1 to 2048 neighbouring positions
- value_experts: int32 [2, 2, 4096, 4, 2], P(None, 'batch', 'seq'), may hold values from 0 to 4, all different within a row
- out_experts: int32 [2, 2, 4096, 4, 2], P(None, 'batch', 'seq'), may hold values from 0 to 4, all different within a row
- norm_gain: bfloat16 [1024], replicated, may hold values from 0.099609375 to 1.8984375
- w_query: bfloat16 [1024, 448], replicated, may hold values from -0.375 to 0.375
- w_key: bfloat16 [1024, 448], replicated, may hold values from -0.1875 to 0.1875
- w_value: bfloat16 [1024, 2240], replicated, may hold values from -0.1875 to 0.1875
- w_vgate: bfloat16 [1024, 20], replicated, may hold values from -0.125 to 0.125
- w_ogate: bfloat16 [1024, 20], replicated, may hold values from -0.125 to 0.125
- w_out: bfloat16 [2240, 1024], replicated, may hold values from -1.5 to 1.5
- ffn_gain: bfloat16 [1024], replicated, may hold values from 0.099609375 to 1.8984375
- w_up: bfloat16 [1024, 4096], replicated, may hold values from -0.1875 to 0.1875
- w_down: bfloat16 [4096, 1024], replicated, may hold values from -0.125 to 0.125
- cotangent: bfloat16 [2, 2, 4096, 1024], P(None, 'batch', 'seq'), may hold values from -6 to 6
Outputs:
- output: bfloat16 [2, 2, 4096, 1024], P(None, 'batch', 'seq')
- input_grad: bfloat16 [2, 2, 4096, 1024], P(None, 'batch', 'seq')
- norm_gain_grad: float32 [1024], P(('seq', 'batch'))
- w_query_grad: float32 [1024, 448], P(('seq', 'batch'))
- w_key_grad: float32 [1024, 448], P(('seq', 'batch'))
- w_value_grad: float32 [1024, 2240], P(('seq', 'batch'))
- w_vgate_grad: float32 [1024, 20], P(('seq', 'batch'))
- w_ogate_grad: float32 [1024, 20], P(('seq', 'batch'))
- w_out_grad: float32 [2240, 1024], P(None, ('seq', 'batch'))
- ffn_gain_grad: float32 [1024], P(('seq', 'batch'))
- w_up_grad: float32 [1024, 4096], P(('seq', 'batch'))
- w_down_grad: float32 [4096, 1024], P(('seq', 'batch'))
Inputs may be any that keep to these rules, and one draw needn't show every extreme that they name: `segments`: in each stream the document numbers never fall; a document has 1 to 2048 positions and some document exactly 2048. `value_experts`: two different experts for each token and head; every expert is chosen somewhere. `out_experts`: two different experts for each token and head; every expert is chosen somewhere.
All inputs are finite; a program needn't handle non-finite values.
Results may differ from a plain program's by a relative error of at most 0.017.
Values may be sent and summed in bfloat16 or wider, within the bound.
No kernel may reach another device: no remote copies, remote signals or barrier semaphores. Data moves between devices by JAX's collectives and lax.ppermute only.
A program may use at most 192 MiB of HBM per device.

v0:
```python
import math

import jax
import jax.numpy as jnp
from jax import lax
from jax.sharding import PartitionSpec as P

HEADS = 4
HEAD = 112
EXPERTS = 5


eps = 1e-06


def passed_along(value, axis, steps):
    count = lax.axis_size(axis)
    initial, last = (max(0, -steps), min(count, count - steps))
    return lax.ppermute(value, axis, [(source, source + steps) for source in range(initial, last)])


def product(left, right):
    return jnp.dot(left, right, preferred_element_type=jnp.float32)


def product_tn(left, right):
    return lax.dot_general(
        left, right, (((0,), (0,)), ((), ())), preferred_element_type=jnp.float32
    )


def product_nt(left, right):
    return lax.dot_general(
        left, right, (((1,), (1,)), ((), ())), preferred_element_type=jnp.float32
    )


def norm_forward(field, gain):
    factor = lax.rsqrt(jnp.mean(field * field, axis=-1, keepdims=True) + eps)
    return ((field * factor * gain).astype(jnp.bfloat16), factor)


def norm_backward(field, factor, gain, grad):
    weighted = grad * gain
    gain_grad = jnp.sum(grad * field * factor, axis=0)
    field_grad = factor * weighted - field * factor**3 * jnp.mean(
        weighted * field, axis=-1, keepdims=True
    )
    return (field_grad, gain_grad)


def gelu_slope(pre):
    normal_cdf = 0.5 * (1.0 + lax.erf(pre * (1.0 / math.sqrt(2.0))))
    density = jnp.exp(-0.5 * pre * pre) * (1.0 / math.sqrt(2.0 * math.pi))
    return normal_cdf + pre * density


def chosen_mask(picked):
    labels = jnp.arange(EXPERTS, dtype=jnp.int32)
    return jnp.sum(
        (picked[:, :, :, None] == labels[None, None, None, :]).astype(jnp.float32), axis=2
    )


def one_batch(field_in, cot_in, own_segs, prior_segs, value_sel, out_sel, weights):
    gain_one, w_query, w_key, w_value, w_vgate, w_ogate, w_out, gain_two, w_up, w_down = weights
    rows = field_in.shape[0]
    att_scale = HEAD ** (-0.5)
    field = field_in.astype(jnp.float32)
    normed, factor_one = norm_forward(field, gain_one)
    query = product(normed, w_query).astype(jnp.bfloat16)
    keys = product(normed, w_key).astype(jnp.bfloat16)
    value_sig = jax.nn.sigmoid(product(normed, w_vgate)).reshape(rows, HEADS, EXPERTS)
    value_pick = chosen_mask(value_sel)
    value_gates = value_sig * value_pick
    expert_values = product(normed, w_value).reshape(rows, HEADS, EXPERTS, HEAD)
    values = (
        jnp.sum(value_gates[..., None] * expert_values, axis=2)
        .reshape(rows, HEADS * HEAD)
        .astype(jnp.bfloat16)
    )
    mem_keys, mem_values = passed_along((keys, values), "seq", 1)
    key_all = jnp.concatenate([mem_keys, keys], 0).reshape(2 * rows, HEADS, HEAD)
    value_all = jnp.concatenate([mem_values, values], 0).reshape(2 * rows, HEADS, HEAD)
    query_heads = query.reshape(rows, HEADS, HEAD)
    key_segs = jnp.concatenate([prior_segs, own_segs], 0)
    query_place = jnp.arange(rows, dtype=jnp.int32) + rows
    key_place = jnp.arange(2 * rows, dtype=jnp.int32)
    allowed = (own_segs[:, None] == key_segs[None, :]) & (
        key_place[None, :] <= query_place[:, None]
    )
    scores = (
        jnp.einsum("qhd,khd->hqk", query_heads, key_all, preferred_element_type=jnp.float32)
        * att_scale
    )
    scores = jnp.where(allowed[None], scores, -1e30)
    top = jnp.max(scores, axis=-1, keepdims=True)
    expo = jnp.exp(scores - top)
    total = jnp.sum(expo, axis=-1, keepdims=True)
    log_total = top + jnp.log(total)
    probs = expo / total
    attended = jnp.einsum(
        "hqk,khd->qhd", probs.astype(jnp.bfloat16), value_all, preferred_element_type=jnp.float32
    ).astype(jnp.bfloat16)
    out_sig = jax.nn.sigmoid(product(normed, w_ogate)).reshape(rows, HEADS, EXPERTS)
    out_pick = chosen_mask(out_sel)
    out_gates = out_sig * out_pick
    attended_f = attended.astype(jnp.float32)
    mixed = (
        (out_gates[..., None] * attended_f[:, :, None, :])
        .reshape(rows, HEADS * EXPERTS * HEAD)
        .astype(jnp.bfloat16)
    )
    hidden = field + product(mixed, w_out)
    normed_two, factor_two = norm_forward(hidden, gain_two)
    pre = product(normed_two, w_up)
    upper = jax.nn.gelu(pre, approximate=False).astype(jnp.bfloat16)
    result = (hidden + product(upper, w_down)).astype(jnp.bfloat16)
    grad_out = cot_in.astype(jnp.float32)
    d_down = grad_out.astype(jnp.bfloat16)
    grad_w_down = product_tn(upper, d_down)
    d_pre = (product_nt(d_down, w_down) * gelu_slope(pre)).astype(jnp.bfloat16)
    grad_w_up = product_tn(normed_two, d_pre)
    d_normed_two = product_nt(d_pre, w_up)
    d_hidden_norm, grad_gain_two = norm_backward(hidden, factor_two, gain_two, d_normed_two)
    d_hidden = grad_out + d_hidden_norm
    d_branch = d_hidden.astype(jnp.bfloat16)
    grad_w_out = product_tn(mixed, d_branch)
    d_mixed = product_nt(d_branch, w_out).reshape(rows, HEADS, EXPERTS, HEAD)
    d_attended = jnp.sum(out_gates[..., None] * d_mixed, axis=2).astype(jnp.bfloat16)
    d_ogate = jnp.sum(attended_f[:, :, None, :] * d_mixed, axis=3)
    d_ologit = (
        (d_ogate * out_pick * out_sig * (1.0 - out_sig))
        .reshape(rows, HEADS * EXPERTS)
        .astype(jnp.bfloat16)
    )
    grad_w_ogate = product_tn(normed, d_ologit)
    d_normed = product_nt(d_ologit, w_ogate)
    again = (
        jnp.einsum("qhd,khd->hqk", query_heads, key_all, preferred_element_type=jnp.float32)
        * att_scale
    )
    again = jnp.where(allowed[None], again, -1e30)
    probs_again = jnp.exp(again - log_total)
    d_probs = jnp.einsum("qhd,khd->hqk", d_attended, value_all, preferred_element_type=jnp.float32)
    delta = jnp.sum(probs_again * d_probs, axis=-1, keepdims=True)
    d_scores = (probs_again * (d_probs - delta)).astype(jnp.bfloat16)
    d_query = (
        (
            jnp.einsum("hqk,khd->qhd", d_scores, key_all, preferred_element_type=jnp.float32)
            * att_scale
        )
        .reshape(rows, HEADS * HEAD)
        .astype(jnp.bfloat16)
    )
    own_scores = d_scores[:, :, rows:]
    own_probs = probs_again[:, :, rows:].astype(jnp.bfloat16)
    d_key_own = (
        jnp.einsum("hqk,qhd->khd", own_scores, query_heads, preferred_element_type=jnp.float32)
        * att_scale
    )
    d_value_own = jnp.einsum(
        "hqk,qhd->khd", own_probs, d_attended, preferred_element_type=jnp.float32
    )
    d_keys = d_key_own.reshape(rows, HEADS * HEAD).astype(jnp.bfloat16)
    d_values = d_value_own.astype(jnp.bfloat16)
    grad_w_query = product_tn(normed, d_query)
    grad_w_key = product_tn(normed, d_keys)
    d_normed = d_normed + product_nt(d_query, w_query) + product_nt(d_keys, w_key)
    d_values_f = d_values.astype(jnp.float32)
    d_expert = (
        (value_gates[..., None] * d_values_f[:, :, None, :])
        .reshape(rows, HEADS * EXPERTS * HEAD)
        .astype(jnp.bfloat16)
    )
    d_vgate = jnp.sum(expert_values * d_values_f[:, :, None, :], axis=3)
    d_vlogit = (
        (d_vgate * value_pick * value_sig * (1.0 - value_sig))
        .reshape(rows, HEADS * EXPERTS)
        .astype(jnp.bfloat16)
    )
    grad_w_value = product_tn(normed, d_expert)
    grad_w_vgate = product_tn(normed, d_vlogit)
    d_normed = d_normed + product_nt(d_expert, w_value) + product_nt(d_vlogit, w_vgate)
    d_field_norm, grad_gain_one = norm_backward(field, factor_one, gain_one, d_normed)
    field_grad = (d_hidden + d_field_norm).astype(jnp.bfloat16)
    grads = (
        grad_gain_one,
        grad_w_query,
        grad_w_key,
        grad_w_value,
        grad_w_vgate,
        grad_w_ogate,
        grad_w_out,
        grad_gain_two,
        grad_w_up,
        grad_w_down,
    )
    return (result, field_grad, grads)


def body(
    tokens,
    segments,
    value_experts,
    out_experts,
    norm_gain,
    w_query,
    w_key,
    w_value,
    w_vgate,
    w_ogate,
    w_out,
    ffn_gain,
    w_up,
    w_down,
    cotangent,
):
    micro = tokens.shape[0]
    block = tokens.shape[2]
    place = lax.axis_index("seq")
    own_all = lax.dynamic_slice_in_dim(segments, place * block, block, 2)
    prior_start = jnp.maximum(place - 1, 0) * block
    prior_all = jnp.where(place > 0, lax.dynamic_slice_in_dim(segments, prior_start, block, 2), -1)
    weights = (
        norm_gain.astype(jnp.float32),
        w_query,
        w_key,
        w_value,
        w_vgate,
        w_ogate,
        w_out,
        ffn_gain.astype(jnp.float32),
        w_up,
        w_down,
    )
    results = []
    field_grads = []
    totals = None
    for step in range(micro):
        result, field_grad, grads = one_batch(
            tokens[step, 0],
            cotangent[step, 0],
            own_all[step, 0],
            prior_all[step, 0],
            value_experts[step, 0],
            out_experts[step, 0],
            weights,
        )
        results.append(result)
        field_grads.append(field_grad)
        if totals is None:
            totals = grads
        else:
            totals = tuple((a + b for a, b in zip(totals, grads)))
    totals = (
        lax.psum_scatter(totals[0], ("seq", "batch"), scatter_dimension=0, tiled=True),
        lax.psum_scatter(totals[1], ("seq", "batch"), scatter_dimension=0, tiled=True),
        lax.psum_scatter(totals[2], ("seq", "batch"), scatter_dimension=0, tiled=True),
        lax.psum_scatter(totals[3], ("seq", "batch"), scatter_dimension=0, tiled=True),
        lax.psum_scatter(totals[4], ("seq", "batch"), scatter_dimension=0, tiled=True),
        lax.psum_scatter(totals[5], ("seq", "batch"), scatter_dimension=0, tiled=True),
        lax.psum_scatter(totals[6], ("seq", "batch"), scatter_dimension=1, tiled=True),
        lax.psum_scatter(totals[7], ("seq", "batch"), scatter_dimension=0, tiled=True),
        lax.psum_scatter(totals[8], ("seq", "batch"), scatter_dimension=0, tiled=True),
        lax.psum_scatter(totals[9], ("seq", "batch"), scatter_dimension=0, tiled=True),
    )
    output = jnp.stack(results, 0)[:, None]
    input_grad = jnp.stack(field_grads, 0)[:, None]
    return (
        output,
        input_grad,
        totals[0],
        totals[1],
        totals[2],
        totals[3],
        totals[4],
        totals[5],
        totals[6],
        totals[7],
        totals[8],
        totals[9],
    )


def solution(mesh):
    placed = (
        P(None, "batch", "seq", None),
        P(None, "batch", None),
        P(None, "batch", "seq", None, None),
        P(None, "batch", "seq", None, None),
        P(),
        P(),
        P(),
        P(),
        P(),
        P(),
        P(),
        P(),
        P(),
        P(),
        P(None, "batch", "seq", None),
    )
    return jax.shard_map(
        body,
        mesh=mesh,
        in_specs=placed,
        out_specs=(
            P(None, "batch", "seq", None),
            P(None, "batch", "seq", None),
            P(("seq", "batch")),
            P(("seq", "batch"), None),
            P(("seq", "batch"), None),
            P(("seq", "batch"), None),
            P(("seq", "batch"), None),
            P(("seq", "batch"), None),
            P(None, ("seq", "batch")),
            P(("seq", "batch")),
            P(("seq", "batch"), None),
            P(("seq", "batch"), None),
        ),
        check_vma=False,
    )
```

profile of v0, /device:TPU:0, one launch (start us, length us, event | category | flops | bytes accessed | tf_op | source)
XLA Modules:
  0.0 1702.6 jit_solution(1530882589458184247)
XLA Ops:
  12.9 6.2 multiply_reduce_fusion.6
  19.2 3.0 collective-permute-start.2
  23.4 4.5 collective-permute-start.3
  29.1 5.9 multiply_reduce_fusion.7
  38.3 3.5 collective-permute-start.1
  63.0 12.9 fusion.7
  75.9 6.4 fusion.1
  85.0 13.3 fusion.4
  98.3 5.9 fusion
  104.3 3.3 multiply_reduce_fusion.11
  108.2 4.5 fusion.127
  121.4 3.2 multiply_reduce_fusion
  128.7 3.8 fusion.131
  166.1 3.7 convolution_add_fusion.5
  177.1 5.2 convolution_add_fusion.3
  182.4 3.1 fusion.129
  185.6 5.2 convolution_add_fusion.2
  190.9 4.4 fusion.139
  195.3 10.2 convolution_add_fusion.1
  206.0 4.1 fusion.108
  210.0 9.9 convolution_add_fusion
  221.9 3.9 fusion.163
  232.0 40.1 %all-reduce.2 = (f32[1024]{0:T(1024)S(1)}, f32[1024]{0:T(1024)S(1)}) all-reduce(f32[1024]{0:T(1024)S(1)} %add.232, f32[1024]{0:T(1024)S(1)} %add.239), channel_id=2, replica_groups=mesh['seq'=16,'batch'=2] {'seq','batch'}, use_global_device_ids=true, to_apply=%region_28.29.clone | all-reduce | flops 2048 | bytes 16384
  273.2 6.5 fusion.48
  279.9 6.0 fusion.49
  291.7 131.0 %reduce-scatter.27.cloned.1.call-done = f32[32,20]{1,0:T(8,128)} async-done(((f32[1024,20]{1,0:T(8,128)}), f32[32,20]{1,0:T(8,128)}) %reduce-scatter.27.cloned.1.call-update) | async-done | bytes 2576
  424.0 135.0 %reduce-scatter.13.cloned.1.call-done = f32[32,448]{1,0:T(8,128)} async-done(((f32[1024,448]{1,0:T(8,128)}), f32[32,448]{1,0:T(8,128)}) %reduce-scatter.13.cloned.1.call-update) | async-done | bytes 57360 | tf_op jit(solution)/shard_map/reduce_scatter | solution.py:258
  559.0 136.0 %reduce-scatter.15.cloned.1.call-done = f32[32,448]{1,0:T(8,128)} async-done(((f32[1024,448]{1,0:T(8,128)}), f32[32,448]{1,0:T(8,128)}) %reduce-scatter.15.cloned.1.call-update) | async-done | bytes 57360 | tf_op jit(solution)/shard_map/reduce_scatter | solution.py:259
  695.1 137.7 %reduce-scatter.17.cloned.1.call-done = f32[32,2240]{1,0:T(8,128)} async-done(((f32[1024,2240]{1,0:T(8,128)}), f32[32,2240]{1,0:T(8,128)}) %reduce-scatter.17.cloned.1.call-update) | async-done | bytes 286736 | tf_op jit(solution)/shard_map/reduce_scatter | solution.py:260
  832.8 142.0 %reduce-scatter.19.cloned.1.call-done = f32[2240,32]{0,1:T(8,128)} async-done(((f32[2240,1024]{0,1:T(8,128)}), f32[2240,32]{0,1:T(8,128)}) %reduce-scatter.19.cloned.1.call-update) | async-done | bytes 286736 | tf_op jit(solution)/shard_map/reduce_scatter | solution.py:263
  974.8 359.2 %reduce-scatter.21.cloned.1.call-done = f32[32,4096]{1,0:T(8,128)} async-done(((f32[1024,4096]{1,0:T(8,128)}), f32[32,4096]{1,0:T(8,128)}) %reduce-scatter.21.cloned.1.call-update) | async-done | bytes 524304 | tf_op jit(solution)/shard_map/reduce_scatter | solution.py:265
  1334.1 361.5 %reduce-scatter.23.cloned.1.call-done = f32[128,1024]{1,0:T(8,128)} async-done(((f32[4096,1024]{1,0:T(8,128)}), f32[128,1024]{1,0:T(8,128)}) %reduce-scatter.23.cloned.1.call-update) | async-done | bytes 524304 | tf_op jit(solution)/shard_map/reduce_scatter | solution.py:266
  (341 shorter events, 105.1 us)
Async XLA Ops:
  7.2 34.6 %copy-start = (bf16[1024,448]{0,1:T(8,128)(2,1)S(1)}, bf16[1024,448]{0,1:T(8,128)(2,1)}, u32[]{:S(2)}) copy-start(bf16[1024,448]{0,1:T(8,128)(2,1)} %param.20) | copy-start | bytes 2752516
  7.2 283.1 %reduce-scatter.25.cloned.1.call-start = ((), (), s32[]{:S(2)}) async-start(), calls=%async_computation.14 | async-start | bytes 540672
  10.8 32.0 %copy-start.78 = (f32[256]{0:T(256)}, f32[256]{0:T(256)S(1)}, u32[]{:S(2)}) copy-start(f32[256]{0:T(256)S(1)} %get-tuple-element.115) | copy-start | bytes 3076
  12.8 9.4 copy-start.1
  12.9 9.3 copy-start.13
  12.9 10.5 copy-start.70
  12.9 15.3 copy-start.60
  19.2 29.4 %collective-permute-start.2 = (bf16[256,448]{0,1:T(8,128)(2,1)}, bf16[256,448]{0,1:T(8,128)(2,1)}, u32[]{:S(2)}, u32[]{:S(2)}) collective-permute-start(bf16[256,448]{0,1:T(8,128)(2,1)} %bitcast.24), channel_id=1, source_target_pairs={{0,2},{2,4},{4,6},{6,8},{8,10},{10,12},{12,14},{14,16},{16,18},{18... | collective-permute-start | bytes 688136 | tf_op jit(solution)/shard_map/ppermute | solution.py:19
  23.4 22.7 %collective-permute-start.3 = (bf16[256,448]{0,1:T(8,128)(2,1)}, bf16[256,448]{0,1:T(8,128)(2,1)}, u32[]{:S(2)}, u32[]{:S(2)}) collective-permute-start(bf16[256,448]{0,1:T(8,128)(2,1)} %convolution_convert_fusion.3), channel_id=1, source_target_pairs={{0,2},{2,4},{4,6},{6,8},{8,10},{10,12},{12,14},{14,16},{16,18},{18... | collective-permute-start | bytes 688136 | tf_op jit(solution)/shard_map/ppermute | solution.py:19
  29.1 9.2 copy-start.69
  35.0 7.8 copy-start.49
  35.0 9.1 copy-start.84
  35.0 21.5 %collective-permute-start = (bf16[256,448]{0,1:T(8,128)(2,1)}, bf16[256,448]{0,1:T(8,128)(2,1)}, u32[]{:S(2)}, u32[]{:S(2)}) collective-permute-start(bf16[256,448]{0,1:T(8,128)(2,1)} %bitcast.8), channel_id=1, source_target_pairs={{0,2},{2,4},{4,6},{6,8},{8,10},{10,12},{12,14},{14,16},{16,18},{18... | collective-permute-start | bytes 688136 | tf_op jit(solution)/shard_map/ppermute | solution.py:19
  38.3 14.8 collective-permute-start.1
  42.8 11.7 copy-start.43
  43.2 8.0 copy-start.73
  43.5 7.7 copy-start.58
  45.1 14.3 copy-start.51
  53.0 54.6 %copy-start.15 = (f32[256,1024]{1,0:T(8,128)}, f32[256,1024]{1,0:T(8,128)S(1)}, u32[]{:S(2)}) copy-start(f32[256,1024]{1,0:T(8,128)S(1)} %get-tuple-element.127) | copy-start | bytes 3145732
  53.0 54.6 %copy-start.82 = (f32[256]{0:T(256)}, f32[256]{0:T(256)S(1)}, u32[]{:S(2)}) copy-start(f32[256]{0:T(256)S(1)} %get-tuple-element.119) | copy-start | bytes 3076
  61.2 46.4 %copy-start.18 = (f32[256,1024]{1,0:T(8,128)}, f32[256,1024]{1,0:T(8,128)S(1)}, u32[]{:S(2)}) copy-start(f32[256,1024]{1,0:T(8,128)S(1)} %get-tuple-element.135) | copy-start | bytes 3145732
  63.0 12.9 copy-start.27
  108.2 20.5 %copy-start.11 = (f32[256,1024]{1,0:T(8,128)}, f32[256,1024]{1,0:T(8,128)S(1)}, u32[]{:S(2)}) copy-start(f32[256,1024]{1,0:T(8,128)S(1)} %get-tuple-element.96) | copy-start | bytes 3145732
  156.5 266.1 %reduce-scatter.27.cloned.1.call-start = ((), (), s32[]{:S(2)}) async-start(), calls=%async_computation.15 | async-start | bytes 540672
  157.4 7.2 copy-start.29
  165.8 393.2 %reduce-scatter.13.cloned.1.call-start = ((), (), s32[]{:S(2)}) async-start(), calls=%async_computation.8 | async-start | bytes 2162688 | tf_op jit(solution)/shard_map/reduce_scatter | solution.py:258
  169.8 525.3 %reduce-scatter.15.cloned.1.call-start = ((), (), s32[]{:S(2)}) async-start(), calls=%async_computation.9 | async-start | bytes 2162688 | tf_op jit(solution)/shard_map/reduce_scatter | solution.py:259
  175.4 657.4 %reduce-scatter.17.cloned.1.call-start = ((), (), s32[]{:S(2)}) async-start(), calls=%async_computation.10 | async-start | bytes 9732096 | tf_op jit(solution)/shard_map/reduce_scatter | solution.py:260
  182.4 792.4 %reduce-scatter.19.cloned.1.call-start = ((), (), s32[]{:S(2)}) async-start(), calls=%async_computation.11 | async-start | bytes 9732096 | tf_op jit(solution)/shard_map/reduce_scatter | solution.py:263
  190.8 1143.2 %reduce-scatter.21.cloned.1.call-start = ((), (), s32[]{:S(2)}) async-start(), calls=%async_computation.12 | async-start | bytes 17301504 | tf_op jit(solution)/shard_map/reduce_scatter | solution.py:265
  205.5 1490.0 %reduce-scatter.23.cloned.1.call-start = ((), (), s32[]{:S(2)}) async-start(), calls=%async_computation.13 | async-start | bytes 17301504 | tf_op jit(solution)/shard_map/reduce_scatter | solution.py:266
  228.9 44.3 %copy-start.16 = (f32[256,1024]{1,0:T(8,128)S(1)}, f32[256,1024]{1,0:T(8,128)}, u32[]{:S(2)}) copy-start(f32[256,1024]{1,0:T(8,128)} %copy-done.15) | copy-start | bytes 3145732
  (77 other events, 273.3 us)
Sparse Core Ops, SparseCore 0:
  156.6 133.5 reduce-scatter.24
  292.6 129.9 reduce-scatter.26
  425.5 133.5 reduce-scatter.12
  561.8 133.1 reduce-scatter.14
  701.4 131.3 reduce-scatter.16
  840.1 134.6 reduce-scatter.18
  977.7 356.3 reduce-scatter.20
  1336.9 358.5 reduce-scatter.22
where the time goes:
time: 1710 us; the launch traced here: 1700 us
  waiting for transfers between devices  1400 us (82%)
  matrix products  170 us (10%)
  blocking collectives  40.1 us (2%)
  other arithmetic  31.6 us (2%)
  local copies, waits for them, and re-layouts  26.2 us (2%)
    reduce_scatter x1, waiting for transfers between devices, body(): lax.psum_scatter(totals[9], ('seq', 'batch'), scatter_dimension=0, tiled=...  361 us
    reduce_scatter x1, waiting for transfers between devices, body(): lax.psum_scatter(totals[8], ('seq', 'batch'), scatter_dimension=0, tiled=...  359 us
    reduce_scatter x1, waiting for transfers between devices, body(): lax.psum_scatter(totals[6], ('seq', 'batch'), scatter_dimension=1, tiled=...  142 us
    reduce_scatter x1, waiting for transfers between devices, body(): lax.psum_scatter(totals[3], ('seq', 'batch'), scatter_dimension=0, tiled=...  138 us
    reduce_scatter x1, waiting for transfers between devices, body(): lax.psum_scatter(totals[2], ('seq', 'batch'), scatter_dimension=0, tiled=...  136 us
    reduce_scatter x1, waiting for transfers between devices, body(): lax.psum_scatter(totals[1], ('seq', 'batch'), scatter_dimension=0, tiled=...  135 us
    unnamed x10, waiting for transfers between devices  133 us
    dot_general x16, matrix products, product(): return jnp.dot(left, right, preferred_element_type=jnp.float32)  59.5 us
  transfers between devices with their start and end apart: 12, of which 8 were waited for; matrix products, arithmetic and copies ran while one was open for 7% of the time, Pallas kernels for 0%

commit v1 on v0

v1 whole, which is shorter than its diff:
```python
import math

import jax
import jax.numpy as jnp
from jax import lax
from jax.sharding import PartitionSpec as P

HEADS = 4
HEAD = 112
EXPERTS = 5

eps = 1e-06


def product(left, right):
    return jnp.dot(left, right, preferred_element_type=jnp.float32)


def product_tn(left, right):
    return lax.dot_general(
        left, right, (((0,), (0,)), ((), ())), preferred_element_type=jnp.float32
    )


def product_nt(left, right):
    return lax.dot_general(
        left, right, (((1,), (1,)), ((), ())), preferred_element_type=jnp.float32
    )


def passed_along(value, axis, steps):
    count = lax.axis_size(axis)
    initial, last = (max(0, -steps), min(count, count - steps))
    return lax.ppermute(value, axis, [(source, source + steps) for source in range(initial, last)])


class Grid:
    def __init__(self):
        self.sizes = {"seq": lax.axis_size("seq"), "batch": lax.axis_size("batch")}
        self.bits = []
        for axis in ("seq", "batch"):
            count = self.sizes[axis].bit_length() - 1
            self.bits += [(axis, at) for at in reversed(range(count))]
        self.index = {"seq": lax.axis_index("seq"), "batch": lax.axis_index("batch")}

    def mine(self, bit):
        axis, at = bit
        return (self.index[axis] >> at) & 1

    def swap(self, value, bit):
        axis, at = bit
        return lax.ppermute(
            value, axis, [(i, i ^ (1 << at)) for i in range(self.sizes[axis])]
        )


class Shards:
    def __init__(self, array, bits):
        self.array, self.bits = array, list(bits)

    def pick(self, bit, value):
        at = self.bits.index(bit)
        rest = self.bits[:at] + self.bits[at + 1 :]
        return Shards(lax.dynamic_index_in_dim(self.array, value, at, keepdims=False), rest)

    def map(self, f):
        return Shards(f(self.array), self.bits)


def flat_rows(array, tail):
    return array.reshape((-1,) + array.shape[array.ndim - tail :])


def reduce_pair(grid, parts, bit):
    mine = grid.mine(bit)
    sent = parts(1 - mine).map(lambda a: a.astype(jnp.bfloat16))
    came = Shards(grid.swap(sent.array, bit), sent.bits)
    return came, (lambda: parts(mine))


def norm_forward(field, gain):
    factor = lax.rsqrt(jnp.mean(field * field, axis=-1, keepdims=True) + eps)
    return ((field * factor * gain).astype(jnp.bfloat16), factor)


def norm_backward(field, factor, gain, grad):
    weighted = grad * gain
    gain_grad = jnp.sum(grad * field * factor, axis=0)
    field_grad = factor * weighted - field * factor**3 * jnp.mean(
        weighted * field, axis=-1, keepdims=True
    )
    return (field_grad, gain_grad)


def chosen_mask(picked):
    labels = jnp.arange(EXPERTS, dtype=jnp.int32)
    return jnp.sum(
        (picked[:, :, :, None] == labels[None, None, None, :]).astype(jnp.float32), axis=2
    )


def core_stage(grid, left, right, extra=None):
    bit = ("seq", 0)
    mine = grid.mine(bit)

    def partial(chosen, columns=None, extra_part=None):
        shape = chosen.array.shape
        out = product(chosen.array.reshape(-1, shape[-1]), right if columns is None else right[:, columns])
        out = out.reshape(shape[:-1] + (out.shape[-1],))
        if extra_part is not None:
            out = out + extra_part.array
        return out

    theirs = left.pick(bit, 1 - mine)
    extra_theirs = None if extra is None else extra.pick(bit, 1 - mine)
    sent = partial(theirs, None, extra_theirs).astype(jnp.bfloat16)
    came = Shards(grid.swap(sent, bit), theirs.bits)
    own = left.pick(bit, mine)
    extra_own = None if extra is None else extra.pick(bit, mine)
    return own, came, extra_own, partial


def plane_stage(grid, staged, first, second, columns):
    own, came, extra, partial = staged
    mine = grid.mine(first)

    def half(value):
        chosen, arrived = own.pick(first, value), came.pick(first, value)
        part = None if extra is None else extra.pick(first, value).map(lambda a: a[..., columns])
        total = partial(chosen, columns, part) + arrived.array[..., columns].astype(jnp.float32)
        return Shards(total.astype(jnp.bfloat16), chosen.bits)

    sent = half(1 - mine)
    arrived = Shards(grid.swap(sent.array, first), sent.bits)
    kept = half(mine)
    return halve(grid, kept, arrived, second)


def halve(grid, kept, arrived, bit):
    mine = grid.mine(bit)

    def half(value):
        a, b = kept.pick(bit, value), arrived.pick(bit, value)
        return Shards(
            (a.array.astype(jnp.float32) + b.array.astype(jnp.float32)).astype(jnp.bfloat16), a.bits
        )

    sent = half(1 - mine)
    return half(mine), Shards(grid.swap(sent.array, bit), sent.bits)


def rest_stages(grid, pair, bits):
    kept, arrived = pair
    for bit in bits:
        kept, arrived = halve(grid, kept, arrived, bit)
    return kept.array.astype(jnp.float32) + arrived.array.astype(jnp.float32)


def joined(pairs):
    kept = Shards(jnp.stack([p[0].array for p in pairs], len(pairs[0][0].bits)), pairs[0][0].bits)
    came = Shards(jnp.stack([p[1].array for p in pairs], len(pairs[0][1].bits)), pairs[0][1].bits)
    return kept, came


def body(
    tokens,
    segments,
    value_experts,
    out_experts,
    norm_gain,
    w_query,
    w_key,
    w_value,
    w_vgate,
    w_ogate,
    w_out,
    ffn_gain,
    w_up,
    w_down,
    cotangent,
):
    grid = Grid()
    bits = grid.bits
    cube = (2,) * len(bits)
    core, plane_a, plane_b = ("seq", 0), ("batch", 0), ("seq", 1)
    rest = [b for b in reversed(bits) if b not in (core, plane_a, plane_b)]
    micro, _, block, width = tokens.shape
    rows = micro * block
    hidden_units = w_up.shape[1]
    place = lax.axis_index("seq")
    own_segs = lax.dynamic_slice_in_dim(segments, place * block, block, 2)[:, 0]
    prior_start = jnp.maximum(place - 1, 0) * block
    prior_segs = jnp.where(
        place > 0, lax.dynamic_slice_in_dim(segments, prior_start, block, 2)[:, 0], -1
    )
    gain_one, gain_two = norm_gain.astype(jnp.float32), ffn_gain.astype(jnp.float32)
    att_scale = HEAD ** (-0.5)

    field = tokens.reshape(rows, width).astype(jnp.float32)
    normed, factor_one = norm_forward(field, gain_one)
    keys = product(normed, w_key).astype(jnp.bfloat16)
    value_sig = jax.nn.sigmoid(product(normed, w_vgate)).reshape(rows, HEADS, EXPERTS)
    value_pick = chosen_mask(value_experts.reshape(rows, HEADS, 2))
    value_gates = value_sig * value_pick
    expert_values = product(normed, w_value).reshape(rows, HEADS, EXPERTS, HEAD)
    values = (
        jnp.sum(value_gates[..., None] * expert_values, axis=2)
        .reshape(rows, HEADS * HEAD)
        .astype(jnp.bfloat16)
    )
    mem_keys, mem_values = passed_along((keys, values), "seq", 1)
    query = product(normed, w_query).astype(jnp.bfloat16)
    split = (micro, block, HEADS, HEAD)
    key_all = jnp.concatenate([mem_keys.reshape(split), keys.reshape(split)], 1)
    value_all = jnp.concatenate([mem_values.reshape(split), values.reshape(split)], 1)
    query_heads = query.reshape(split)
    key_segs = jnp.concatenate([prior_segs, own_segs], 1)
    query_place = jnp.arange(block, dtype=jnp.int32) + block
    key_place = jnp.arange(2 * block, dtype=jnp.int32)
    allowed = (own_segs[:, :, None] == key_segs[:, None, :]) & (
        key_place[None, None, :] <= query_place[None, :, None]
    )
    scores = (
        jnp.einsum("mqhd,mkhd->mhqk", query_heads, key_all, preferred_element_type=jnp.float32)
        * att_scale
    )
    scores = jnp.where(allowed[:, None], scores, -1e30)
    top = jnp.max(scores, axis=-1, keepdims=True)
    expo = jnp.exp(scores - top)
    probs = expo / jnp.sum(expo, axis=-1, keepdims=True)
    probs_low = probs.astype(jnp.bfloat16)
    attended = (
        jnp.einsum("mhqk,mkhd->mqhd", probs_low, value_all, preferred_element_type=jnp.float32)
        .astype(jnp.bfloat16)
        .reshape(rows, HEADS, HEAD)
    )
    out_sig = jax.nn.sigmoid(product(normed, w_ogate)).reshape(rows, HEADS, EXPERTS)
    out_pick = chosen_mask(out_experts.reshape(rows, HEADS, 2))
    out_gates = out_sig * out_pick
    attended_f = attended.astype(jnp.float32)
    mixed = (
        (out_gates[..., None] * attended_f[:, :, None, :])
        .reshape(rows, HEADS * EXPERTS * HEAD)
        .astype(jnp.bfloat16)
    )
    hidden = field + product(mixed, w_out)
    normed_two, factor_two = norm_forward(hidden, gain_two)
    pre = product(normed_two, w_up)
    cdf = 0.5 * (1.0 + lax.erf(pre * (1.0 / math.sqrt(2.0))))
    upper = (pre * cdf).astype(jnp.bfloat16)
    slope = cdf + pre * (jnp.exp(-0.5 * pre * pre) * (1.0 / math.sqrt(2.0 * math.pi)))
    d_down = cotangent.reshape(rows, width)
    grad_out = d_down.astype(jnp.float32)

    upper_t = Shards(upper.T.reshape(cube + (-1, rows)), bits)
    staged_down = core_stage(grid, upper_t, d_down)
    d_pre = (product_nt(d_down, w_down) * slope).astype(jnp.bfloat16)
    normed_two_t = Shards(normed_two.T.reshape(cube + (-1, rows)), bits)
    staged_up = core_stage(grid, normed_two_t, d_pre)
    half = width // 2
    down_a = plane_stage(grid, staged_down, plane_a, plane_b, slice(0, half))
    down_b = plane_stage(grid, staged_down, plane_b, plane_a, slice(half, width))
    half = hidden_units // 2
    up_a = plane_stage(grid, staged_up, plane_a, plane_b, slice(0, half))
    up_b = plane_stage(grid, staged_up, plane_b, plane_a, slice(half, hidden_units))
    d_normed_two = product_nt(d_pre, w_up)
    d_hidden_norm, grad_gain_two = norm_backward(hidden, factor_two, gain_two, d_normed_two)
    d_hidden = grad_out + d_hidden_norm
    d_branch = d_hidden.astype(jnp.bfloat16)
    branch_t = Shards(d_branch.T.reshape(cube + (-1, rows)), bits)
    staged_out = core_stage(grid, branch_t, mixed)
    d_mixed = product_nt(d_branch, w_out).reshape(rows, HEADS, EXPERTS, HEAD)
    out_pair = plane_stage(grid, staged_out, plane_a, plane_b, slice(0, mixed.shape[1]))
    result = (hidden + product(upper, w_down)).astype(jnp.bfloat16)
    d_attended = jnp.sum(out_gates[..., None] * d_mixed, axis=2).astype(jnp.bfloat16)
    d_ogate = jnp.sum(attended_f[:, :, None, :] * d_mixed, axis=3)
    d_ologit = (
        (d_ogate * out_pick * out_sig * (1.0 - out_sig))
        .reshape(rows, HEADS * EXPERTS)
        .astype(jnp.bfloat16)
    )
    d_attended = d_attended.reshape(split)
    d_probs = jnp.einsum(
        "mqhd,mkhd->mhqk", d_attended, value_all, preferred_element_type=jnp.float32
    )
    delta = jnp.sum(probs * d_probs, axis=-1, keepdims=True)
    d_scores = (probs * (d_probs - delta)).astype(jnp.bfloat16)
    d_query = (
        (
            jnp.einsum("mhqk,mkhd->mqhd", d_scores, key_all, preferred_element_type=jnp.float32)
            * att_scale
        )
        .reshape(rows, HEADS * HEAD)
        .astype(jnp.bfloat16)
    )
    d_keys = (
        (
            jnp.einsum(
                "mhqk,mqhd->mkhd",
                d_scores[..., block:],
                query_heads,
                preferred_element_type=jnp.float32,
            )
            * att_scale
        )
        .reshape(rows, HEADS * HEAD)
        .astype(jnp.bfloat16)
    )
    d_values = (
        jnp.einsum(
            "mhqk,mqhd->mkhd",
            probs_low[..., block:],
            d_attended,
            preferred_element_type=jnp.float32,
        )
        .astype(jnp.bfloat16)
        .reshape(rows, HEADS, HEAD)
    )
    d_values_f = d_values.astype(jnp.float32)
    d_expert = (
        (value_gates[..., None] * d_values_f[:, :, None, :])
        .reshape(rows, HEADS * EXPERTS * HEAD)
        .astype(jnp.bfloat16)
    )
    d_vgate = jnp.sum(expert_values * d_values_f[:, :, None, :], axis=3)
    d_vlogit = (
        (d_vgate * value_pick * value_sig * (1.0 - value_sig))
        .reshape(rows, HEADS * EXPERTS)
        .astype(jnp.bfloat16)
    )
    d_normed = (
        product_nt(d_ologit, w_ogate)
        + product_nt(d_query, w_query)
        + product_nt(d_keys, w_key)
        + product_nt(d_expert, w_value)
        + product_nt(d_vlogit, w_vgate)
    )
    d_field_norm, grad_gain_one = norm_backward(field, factor_one, gain_one, d_normed)
    field_grad = (d_hidden + d_field_norm).astype(jnp.bfloat16)

    wide = jnp.concatenate([d_query, d_keys, d_expert, d_vlogit, d_ologit], 1)
    used = wide.shape[1]
    full = -(-(used + 2) // 128) * 128
    wide = jnp.pad(wide, ((0, 0), (0, full - used)))
    gains = jnp.stack([grad_gain_one, grad_gain_two], 1)
    gains = jnp.pad(gains, ((0, 0), (used, full - used - 2)))
    gains = Shards(gains.reshape(cube + (-1, full)), bits)
    normed_t = Shards(normed.T.reshape(cube + (-1, rows)), bits)
    staged_in = core_stage(grid, normed_t, wide, gains)
    in_pair = plane_stage(grid, staged_in, plane_b, plane_a, slice(0, full))

    down = rest_stages(grid, joined([down_a, down_b]), rest)
    grad_down = jnp.concatenate([down[0], down[1]], -1)
    up = rest_stages(grid, joined([up_a, up_b]), rest)
    grad_up = jnp.concatenate([up[0], up[1]], -1)
    grad_out_w = rest_stages(grid, out_pair, rest).T
    grad_in = rest_stages(grid, in_pair, rest)
    pieces = []
    start = 0
    for size in (w_query.shape[1], w_key.shape[1], w_value.shape[1], w_vgate.shape[1], w_ogate.shape[1]):
        pieces.append(grad_in[:, start : start + size])
        start += size
    return (
        result.reshape(tokens.shape),
        field_grad.reshape(tokens.shape),
        grad_in[:, start],
        pieces[0],
        pieces[1],
        pieces[2],
        pieces[3],
        pieces[4],
        grad_out_w,
        grad_in[:, start + 1],
        grad_up,
        grad_down,
    )


def solution(mesh):
    both = ("seq", "batch")
    stream = P(None, "batch", "seq", None)
    picks = P(None, "batch", "seq", None, None)
    return jax.shard_map(
        body,
        mesh=mesh,
        in_specs=(stream, P(None, "batch", None), picks, picks) + (P(),) * 10 + (stream,),
        out_specs=(
            stream,
            stream,
            P(both),
            P(both, None),
            P(both, None),
            P(both, None),
            P(both, None),
            P(both, None),
            P(None, both),
            P(both),
            P(both, None),
            P(both, None),
        ),
        check_vma=False,
    )
```

time: 1710 us -> 426 us (0.25)
  waiting for transfers between devices: 1400 us -> 125 us
  local copies, waits for them, and re-layouts: 26.2 us -> 106 us
  matrix products: 170 us -> 126 us
  blocking collectives: 40.1 us -> 0 us
  starting transfers between devices: 14.2 us -> 32.6 us
    reduce_scatter x6 -> x0, waiting for transfers between devices: 1270 us -> none  [the longest x1 361 us: body(): lax.psum_scatter(totals[9], ('seq', 'batch'), scatter_dimension=0, tiled=...]
    unnamed x10 -> x0, waiting for transfers between devices: 133 us -> none
    ppermute x0 -> x24, waiting for transfers between devices: none -> 125 us  [swap(): lax.ppermute(value, axis, [(i, i ^ 1 << at) for i in range(self.sizes[axi...]
    dot_general x28 -> x6, matrix products: 73.8 us -> 4.87 us  [the longest x1 1.17 us: body(): jnp.einsum('mqhd,mkhd->mhqk', d_attended, value_all, preferred_element_ty...]
    unnamed x1 -> x0, blocking collectives: 40.1 us -> none
    dynamic_slice x0 -> x8, local copies, waits for them, and re-layouts: none -> 40.1 us  [pick(): lax.dynamic_index_in_dim(self.array, value, at, keepdims=False)]
    ppermute x0 -> x24, starting transfers between devices: none -> 24.7 us  [swap(): lax.ppermute(value, axis, [(i, i ^ 1 << at) for i in range(self.sizes[axi...]
    dot_general x16 -> x24, matrix products: 59.5 us -> 76.2 us  [product(): return jnp.dot(left, right, preferred_element_type=jnp.float32)]
  transfers between devices with their start and end apart: 12 -> 26, of which waited for: 8 -> 12; matrix products, arithmetic and copies ran while one was open for 7% -> 32% of each run, Pallas kernels for 0% -> 0%
where the time goes in v1:
time: 426 us; the launch traced here: 420 us
  matrix products  126 us (30%)
  waiting for transfers between devices  125 us (29%)
  local copies, waits for them, and re-layouts  106 us (25%)
  starting transfers between devices  32.6 us (8%)
  other arithmetic  28.2 us (7%)
    ppermute x24, waiting for transfers between devices, swap(): lax.ppermute(value, axis, [(i, i ^ 1 << at) for i in range(self.sizes[axi...  125 us
    dot_general x24, matrix products, product(): return jnp.dot(left, right, preferred_element_type=jnp.float32)  76.2 us
    dot_general x8, matrix products, product_nt(): lax.dot_general(left, right, (((1,), (1,)), ((), ())), preferred_element_...  44.5 us
    dynamic_slice x8, local copies, waits for them, and re-layouts, pick(): lax.dynamic_index_in_dim(self.array, value, at, keepdims=False)  40.1 us
    ppermute x24, starting transfers between devices, swap(): lax.ppermute(value, axis, [(i, i ^ 1 << at) for i in range(self.sizes[axi...  24.7 us
    squeeze x4, local copies, waits for them, and re-layouts, pick(): lax.dynamic_index_in_dim(self.array, value, at, keepdims=False)  11.5 us
  transfers between devices with their start and end apart: 26, of which 12 were waited for; matrix products, arithmetic and copies ran while one was open for 32% of the time, Pallas kernels for 0%

profile of v1, /device:TPU:0, one launch (start us, length us, event | category | flops | bytes accessed | tf_op | source)
XLA Modules:
  0.0 420.3 jit_solution(15855755839748563675)
XLA Ops:
  6.3 8.0 %multiply_reduce_fusion.3 = (bf16[512,4,112]{0,2,1:T(8,128)(2,1)}, f32[512,4,5,112]{0,3,2,1:T(8,128)}) fusion(f32[512,4,5]{0,2,1:T(8,128)S(1)} %copy.200, bf16[512,1024,1,1]{1,0,3,2:T(8,128)(2,1)S(1)} %bitcast.509, bf16[4,5,112,1024]{3,2,1,0:T(8,128)(2,1)} %bitcast.526), kind=kOutput, calls=%fused_computation.26 | convolution fusion | flops 2350874624 | bytes 10723328 | tf_op jit(solution)/shard_map/dot_general | solution.py:16
  18.8 4.8 %collective-permute-start.1 = (bf16[512,448]{0,1:T(8,128)(2,1)}, bf16[512,448]{0,1:T(8,128)(2,1)}, u32[]{:S(2)}, u32[]{:S(2)}) collective-permute-start(bf16[512,448]{0,1:T(8,128)(2,1)} %convolution_convert_fusion.5), channel_id=1, source_target_pairs={{0,2},{2,4},{4,6},{6,8},{8,10},{10,12},{12,14},{14,16},{16,18},{18... | collective-permute-start | bytes 1376264 | tf_op jit(solution)/shard_map/ppermute | solution.py:34
  54.0 8.8 %fusion.10 = (bf16[4096,512]{0,1:T(8,128)(2,1)}, f32[512,4096]{1,0:T(8,128)}) fusion(bf16[1024,4096]{1,0:T(8,128)(2,1)S(1)} %bitcast.523, f32[512,1024]{1,0:T(8,128)S(1)} %get-tuple-element.116, f32[1024]{0:T(1024)S(1)} %convert_element_type.725, f32[512]{0:T(512)S(1)} %get-tuple-element.108), kind=kOutput, calls=%fused_computation.15 | convolution fusion | flops 4307025920 | bytes 23074816 | tf_op jit(solution)/shard_map/dot_general | solution.py:16
  62.8 11.4 %fusion.6 = bf16[512,4096]{1,0:T(8,128)(2,1)} fusion(f32[512,4096]{1,0:T(8,128)} %get-tuple-element.122, bf16[512,1024]{1,0:T(8,128)(2,1)S(1)} %bitcast.504, bf16[4096,1024]{1,0:T(8,128)(2,1)} %param.28), kind=kOutput, calls=%fused_computation.7 | convolution fusion | flops 4315938816 | bytes 22020096 | tf_op jit(solution)/shard_map/dot_general | solution.py:26
  74.2 8.8 %multiply_reduce_fusion.5 = (f32[1024]{0:T(1024)S(1)}, f32[512]{0:T(512)S(1)}, f32[512,1024]{1,0:T(8,128)S(1)}) fusion(f32[512,1024]{1,0:T(8,128)S(1)} %get-tuple-element.116, f32[512]{0:T(512)S(1)} %get-tuple-element.108, f32[1024]{0:T(1024)S(1)} %convert_element_type.725, bf16[512,4096]{1,0:T(8,128)(2,1)} %fusion.6, bf16[1024,4096]{1,0:T(8,128)(2,1)} %param.27), kind=kOutput, calls=%fused_computation.88 | convolution fusion | flops 4298111488 | bytes 16789504 | tf_op jit(solution)/shard_map/dot_general | solution.py:26
  85.2 5.7 %fusion.113 = f32[512,2240]{0,1:T(8,128)S(1)} fusion(bf16[2240,1024]{1,0:T(8,128)(2,1)} %param.25, f32[512,1024]{1,0:T(8,128)S(1)} %get-tuple-element.69), kind=kOutput, calls=%fused_computation.223 | convolution fusion | flops 2349334528 | bytes 11272192 | tf_op jit(solution)/shard_map/dot_general | solution.py:26
  105.6 6.3 %fusion.191 = f32[512,1024]{1,0:T(8,128)} fusion(bf16[512,2240]{0,1:T(8,128)(2,1)S(1)} %bitcast.475, bf16[1024,2240]{0,1:T(8,128)(2,1)} %param.22), kind=kOutput, calls=%fused_computation.337 | convolution fusion | flops 2348810240 | bytes 8978432 | tf_op jit(solution)/shard_map/dot_general | solution.py:26
  111.9 4.3 %copy.220 = bf16[512,2240]{1,0:T(8,128)(2,1)} copy(bf16[512,2240]{0,1:T(8,128)(2,1)} %bitcast.476) | data formatting | bytes 4587520 | tf_op jit(solution)/shard_map/convert_element_type | solution.py:323
  123.2 6.6 %fusion.39 = (f32[1024]{0:T(1024)S(1)}, f32[512]{0:T(512)}, f32[512,1024]{1,0:T(8,128)}) fusion(bf16[2,1,256,1024]{3,2,1,0:T(8,128)(2,1)S(1)} %copy-done.4, f32[512]{0:T(512)S(1)} %bitcast.518, f32[1024]{0:T(1024)S(1)} %convert_element_type.707, f32[512,1024]{1,0:T(8,128)} %fusion.192, f32[512,1024]{1,0:T(8,128)} %fusion.191, ...), kind=kOutput, calls=%fused_computation.71 | convolution fusion | flops 475527680 | bytes 12922880 | tf_op jit(solution)/shard_map/dot_general | solution.py:26
  130.1 5.7 %pad.9.clone = f32[1024,3200]{1,0:T(8,128)} pad(f32[1024,2]{1,0:T(8,128)S(1)} %copy.290, f32[]{:T(128)} %constant.737.clone.1), padding=0_0x3176_22 | pad | bytes 13115396 | tf_op jit(solution)/shard_map/jit(_pad)/pad | solution.py:346
  135.8 6.4 %concatenate.21 = bf16[512,3176]{1,0:T(8,128)(2,1)} concatenate(bf16[512,448]{1,0:T(8,128)(2,1)S(1)} %copy-done.14, bf16[512,448]{1,0:T(8,128)(2,1)S(1)} %copy-done.15, bf16[512,2240]{1,0:T(8,128)(2,1)} %copy.220, bf16[512,20]{1,0:T(8,128)(2,1)S(1)} %copy-done.27, bf16[512,20]{1,0:T(8,128)(2,1)S(1)} %copy-done.28), dimensions={1} | concatenate | bytes 6504448 | tf_op jit(solution)/shard_map/concatenate | solution.py:341
  142.2 7.5 %fusion.11 = bf16[2,2,2,2,32,3200]{5,4,0,3,1,2:T(8,128)(2,1)} fusion(bf16[512,3176]{1,0:T(8,128)(2,1)} %concatenate.21, f32[2,2,2,2,2,32,3200]{6,5,4,3,2,1,0:T(8,128)} %bitcast.465, s32[]{:T(128)S(6)} %select_n.179, bf16[2,2,2,2,2,32,512]{6,5,4,3,2,1,0:T(8,128)(2,1)S(1)} %bitcast.480), kind=kOutput, calls=%fused_computation.17 | convolution fusion | flops 1680998400 | bytes 13632512 | tf_op jit(solution)/shard_map/dot_general | solution.py:16
  152.1 4.6 %convolution_convert_fusion.1 = bf16[2,2,2,2,32,2240]{5,4,0,2,1,3:T(8,128)(2,1)} fusion(bf16[512,2240,1,1,1,1]{0,1,2,4,3,5:T(8,128)(2,1)} %bitcast.471, bf16[2,2,2,2,2,32,512]{6,5,4,3,2,1,0:T(8,128)(2,1)} %bitcast.488, s32[]{:T(128)S(6)} %select_n.179), kind=kOutput, calls=%fused_computation.27 | convolution fusion | flops 1175552000 | bytes 5111812 | tf_op jit(solution)/shard_map/dot_general | solution.py:16
  159.6 6.7 %convolution_convert_fusion = bf16[2,2,2,2,32,4096]{5,4,3,2,1,0:T(8,128)(2,1)} fusion(bf16[512,4096]{1,0:T(8,128)(2,1)} %fusion.6, bf16[2,2,2,2,2,32,512]{6,5,4,3,2,1,0:T(8,128)(2,1)} %bitcast.510, s32[]{:T(128)S(6)} %select_n.179), kind=kOutput, calls=%fused_computation.18 | convolution fusion | flops 2149580800 | bytes 8912900 | tf_op jit(solution)/shard_map/dot_general | solution.py:16
  166.3 7.7 %reshape.524 = bf16[2,2,2,2,2,128,512]{5,4,3,2,1,0,6:T(2,128)(2,1)} reshape(bf16[4096,512]{0,1:T(8,128)(2,1)} %get-tuple-element.121) | data formatting | bytes 8388608 | tf_op jit(solution)/shard_map/reshape | solution.py:255
  174.0 4.4 %constant_dynamic-slice_fusion.1 = bf16[2,2,2,1,2,128,512]{5,4,3,2,1,0,6:T(2,128)(2,1)} fusion(bf16[2,2,2,2,2,128,512]{5,4,3,2,1,0,6:T(2,128)(2,1)} %reshape.524, s32[]{:T(128)S(6)} %select_n.179), kind=kLoop, calls=%fused_computation.292 | loop fusion | bytes 4194308 | tf_op jit(solution)/shard_map/jit(dynamic_index_in_dim)/dynamic_slice | solution.py:64
  178.4 6.1 %copy.245 = bf16[2,2,2,1,2,128,512]{6,5,4,2,1,0,3:T(8,128)(2,1)} copy(bf16[2,2,2,1,2,128,512]{5,4,3,2,1,0,6:T(2,128)(2,1)} %constant_dynamic-slice_fusion.1) | data formatting | bytes 4194304 | tf_op jit(solution)/shard_map/jit(dynamic_index_in_dim)/dynamic_slice | solution.py:64
  184.6 6.3 %convolution_convert_fusion.2 = bf16[2,2,2,2,128,1024]{5,4,3,2,1,0:T(8,128)(2,1)} fusion(bf16[512,1024,1,1,1,1]{1,0,5,4,3,2:T(8,128)(2,1)} %bitcast.503, bf16[2,2,2,1,2,128,512]{6,5,4,2,1,0,3:T(8,128)(2,1)} %copy.245), kind=kOutput, calls=%fused_computation.42 | convolution fusion | flops 2149580800 | bytes 7340032 | tf_op jit(solution)/shard_map/dot_general | solution.py:16
  191.4 6.3 %constant_dynamic-slice_fusion.2 = (bf16[2,2,2,1,1,128,512]{5,4,3,2,1,0,6:T(2,128)(2,1)}, bf16[2,2,2,1,1,128,512]{5,4,3,2,1,0,6:T(2,128)(2,1)}) fusion(bf16[2,2,2,2,2,128,512]{5,4,3,2,1,0,6:T(2,128)(2,1)S(1)} %copy-done.3, s32[]{:T(128)S(6)} %select_n.178, s32[]{:T(128)S(6)} %select_n.188, s32[]{:T(128)S(6)} %select_n.189), kind=kLoop, calls=%fused_computation.293 | loop fusion | bytes 4194316 | tf_op jit(solution)/shard_map/jit(dynamic_index_in_dim)/dynamic_slice | solution.py:64
  197.7 5.8 %copy.246 = bf16[2,2,2,1,1,128,512]{6,5,2,1,0,4,3:T(8,128)(2,1)} copy(bf16[2,2,2,1,1,128,512]{5,4,3,2,1,0,6:T(2,128)(2,1)} %get-tuple-element.75) | data formatting | bytes 2097152 | tf_op jit(solution)/shard_map/jit(dynamic_index_in_dim)/dynamic_slice | solution.py:64
  203.5 5.8 %copy.244 = bf16[2,2,2,1,1,128,512]{6,5,2,1,0,4,3:T(8,128)(2,1)} copy(bf16[2,2,2,1,1,128,512]{5,4,3,2,1,0,6:T(2,128)(2,1)} %get-tuple-element.74) | data formatting | bytes 2097152 | tf_op jit(solution)/shard_map/jit(dynamic_index_in_dim)/dynamic_slice | solution.py:64
  209.3 4.3 %constant_dynamic-slice_fusion.3 = (bf16[2,2,1,1,2,128,512]{5,4,3,2,1,0,6:T(2,128)(2,1)}, bf16[2,2,1,1,2,128,512]{5,4,3,2,1,0,6:T(2,128)(2,1)}) fusion(bf16[2,2,2,2,2,128,512]{5,4,3,2,1,0,6:T(2,128)(2,1)} %reshape.524, s32[]{:T(128)S(6)} %select_n.176, s32[]{:T(128)S(6)} %select_n.178, s32[]{:T(128)S(6)} %select_n.182), kind=kLoop, calls=%fused_computation.299 | loop fusion | bytes 4194316 | tf_op jit(solution)/shard_map/jit(dynamic_index_in_dim)/dynamic_slice | solution.py:64
  221.0 10.8 %add_convert_fusion.8 = bf16[512,1024]{1,0:T(8,128)(2,1)} fusion(f32[512,1024]{1,0:T(8,128)} %copy-done.13, bf16[4096,1024]{1,0:T(8,128)(2,1)} %param.28, f32[512,4096]{1,0:T(8,128)} %get-tuple-element.122), kind=kOutput, calls=%fused_computation.92 | convolution fusion | flops 4306501632 | bytes 19922944 | tf_op jit(solution)/shard_map/dot_general | solution.py:16
  242.8 19.2 %collective-permute-done.8 = bf16[2,2,2,32,2240]{4,3,0,2,1:T(8,128)(2,1)S(1)} collective-permute-done((bf16[2,2,2,32,2240]{4,3,0,2,1:T(8,128)(2,1)S(1)}, bf16[2,2,2,32,2240]{4,3,0,2,1:T(8,128)(2,1)S(1)}, u32[]{:S(2)}, u32[]{:S(2)}) %collective-permute-start.8) | collective-permute-done | bytes 1146912 | tf_op jit(solution)/shard_map/ppermute | solution.py:52
  265.5 26.6 %collective-permute-done.9 = bf16[2,2,32,2240]{3,2,1,0:T(8,128)(2,1)S(1)} collective-permute-done((bf16[2,2,32,2240]{3,2,1,0:T(8,128)(2,1)S(1)}, bf16[2,2,32,2240]{3,2,1,0:T(8,128)(2,1)S(1)}, u32[]{:S(2)}, u32[]{:S(2)}) %collective-permute-start.9) | collective-permute-done | bytes 573472 | tf_op jit(solution)/shard_map/ppermute | solution.py:52
  316.0 5.0 %collective-permute-done.11 = bf16[32,2240]{1,0:T(8,128)(2,1)S(1)} collective-permute-done((bf16[32,2240]{1,0:T(8,128)(2,1)S(1)}, bf16[32,2240]{1,0:T(8,128)(2,1)S(1)}, u32[]{:S(2)}, u32[]{:S(2)}) %collective-permute-start.11) | collective-permute-done | bytes 143392 | tf_op jit(solution)/shard_map/ppermute | solution.py:52
  329.4 16.2 %collective-permute-done.20 = bf16[2,2,2,128,512]{4,3,2,1,0:T(8,128)(2,1)S(1)} collective-permute-done((bf16[2,2,2,128,512]{4,3,2,1,0:T(8,128)(2,1)S(1)}, bf16[2,2,2,128,512]{4,3,2,1,0:T(8,128)(2,1)S(1)}, u32[]{:S(2)}, u32[]{:S(2)}) %collective-permute-start.20) | collective-permute-done | bytes 1048608 | tf_op jit(solution)/shard_map/ppermute | solution.py:52
  351.6 11.6 %collective-permute-done.4 = bf16[2,2,32,3200]{3,2,1,0:T(8,128)(2,1)S(1)} collective-permute-done((bf16[2,2,32,3200]{3,2,1,0:T(8,128)(2,1)S(1)}, bf16[2,2,32,3200]{3,2,1,0:T(8,128)(2,1)S(1)}, u32[]{:S(2)}, u32[]{:S(2)}) %collective-permute-start.4) | collective-permute-done | bytes 819232 | tf_op jit(solution)/shard_map/ppermute | solution.py:52
  364.5 9.9 %collective-permute-done.16 = bf16[2,2,32,2048]{3,2,1,0:T(8,128)(2,1)S(1)} collective-permute-done((bf16[2,2,32,2048]{3,2,1,0:T(8,128)(2,1)S(1)}, bf16[2,2,32,2048]{3,2,1,0:T(8,128)(2,1)S(1)}, u32[]{:S(2)}, u32[]{:S(2)}) %collective-permute-start.16) | collective-permute-done | bytes 524320 | tf_op jit(solution)/shard_map/ppermute | solution.py:52
  375.7 7.5 %collective-permute-done.23 = bf16[2,2,128,512]{3,2,1,0:T(8,128)(2,1)S(1)} collective-permute-done((bf16[2,2,128,512]{3,2,1,0:T(8,128)(2,1)S(1)}, bf16[2,2,128,512]{3,2,1,0:T(8,128)(2,1)S(1)}, u32[]{:S(2)}, u32[]{:S(2)}) %collective-permute-start.23) | collective-permute-done | bytes 524320 | tf_op jit(solution)/shard_map/ppermute | solution.py:52
  388.8 16.2 %collective-permute-done.24 = bf16[2,2,128,512]{3,2,0,1:T(8,128)(2,1)S(1)} collective-permute-done((bf16[2,2,128,512]{3,2,0,1:T(8,128)(2,1)S(1)}, bf16[2,2,128,512]{3,2,0,1:T(8,128)(2,1)S(1)}, u32[]{:S(2)}, u32[]{:S(2)}) %collective-permute-start.24) | collective-permute-done | bytes 524320 | tf_op jit(solution)/shard_map/ppermute | solution.py:52
  412.7 5.4 %collective-permute-done.25 = bf16[2,128,512]{2,1,0:T(8,128)(2,1)S(1)} collective-permute-done((bf16[2,128,512]{2,1,0:T(8,128)(2,1)S(1)}, bf16[2,128,512]{2,1,0:T(8,128)(2,1)S(1)}, u32[]{:S(2)}, u32[]{:S(2)}) %collective-permute-start.25) | collective-permute-done | bytes 262176 | tf_op jit(solution)/shard_map/ppermute | solution.py:52
  (287 shorter events, 147.1 us)
Async XLA Ops:
  0.6 16.7 %copy-start = (bf16[1024,448]{0,1:T(8,128)(2,1)S(1)}, bf16[1024,448]{0,1:T(8,128)(2,1)}, u32[]{:S(2)}) copy-start(bf16[1024,448]{0,1:T(8,128)(2,1)} %param.21) | copy-start | bytes 2752516
  14.3 23.4 %collective-permute-start = (bf16[512,448]{0,1:T(8,128)(2,1)}, bf16[512,448]{0,1:T(8,128)(2,1)}, u32[]{:S(2)}, u32[]{:S(2)}) collective-permute-start(bf16[512,448]{0,1:T(8,128)(2,1)} %bitcast.6), channel_id=1, source_target_pairs={{0,2},{2,4},{4,6},{6,8},{8,10},{10,12},{12,14},{14,16},{16,18},{18... | collective-permute-start | bytes 1376264 | tf_op jit(solution)/shard_map/ppermute | solution.py:34
  18.8 21.8 %collective-permute-start.1 = (bf16[512,448]{0,1:T(8,128)(2,1)}, bf16[512,448]{0,1:T(8,128)(2,1)}, u32[]{:S(2)}, u32[]{:S(2)}) collective-permute-start(bf16[512,448]{0,1:T(8,128)(2,1)} %convolution_convert_fusion.5), channel_id=1, source_target_pairs={{0,2},{2,4},{4,6},{6,8},{8,10},{10,12},{12,14},{14,16},{16,18},{18... | collective-permute-start | bytes 1376264 | tf_op jit(solution)/shard_map/ppermute | solution.py:34
  53.5 29.6 %copy-start.13 = (f32[512,1024]{1,0:T(8,128)}, f32[512,1024]{1,0:T(8,128)S(1)}, u32[]{:S(2)}) copy-start(f32[512,1024]{1,0:T(8,128)S(1)} %get-tuple-element.116) | copy-start | bytes 6291460
  149.7 89.8 %collective-permute-start.2 = (bf16[2,2,2,2,32,3200]{5,4,0,3,1,2:T(8,128)(2,1)}, bf16[2,2,2,2,32,3200]{5,4,0,3,1,2:T(8,128)(2,1)}, u32[]{:S(2)}, u32[]{:S(2)}) collective-permute-start(bf16[2,2,2,2,32,3200]{5,4,0,3,1,2:T(8,128)(2,1)} %fusion.11), channel_id=1, source_target_pairs={{0,2},{2,0},{4,6},{6,4},{8,10},{10,8},{12,14},{14,12},{16,18},{18,... | collective-permute-start | bytes 9830408 | tf_op jit(solution)/shard_map/ppermute | solution.py:52
  156.8 75.0 %collective-permute-start.7 = (bf16[2,2,2,2,32,2240]{5,4,0,2,1,3:T(8,128)(2,1)}, bf16[2,2,2,2,32,2240]{5,4,0,2,1,3:T(8,128)(2,1)}, u32[]{:S(2)}, u32[]{:S(2)}) collective-permute-start(bf16[2,2,2,2,32,2240]{5,4,0,2,1,3:T(8,128)(2,1)} %convolution_convert_fusion.1), channel_id=1, source_target_pairs={{0,2},{2,0},{4,6},{6,4},{8,10},{10,8},{12,14},{14,12},{16,18},{18,... | collective-permute-start | bytes 6881288 | tf_op jit(solution)/shard_map/ppermute | solution.py:52
  166.3 126.9 %collective-permute-start.12 = (bf16[2,2,2,2,32,4096]{5,4,3,2,1,0:T(8,128)(2,1)}, bf16[2,2,2,2,32,4096]{5,4,3,2,1,0:T(8,128)(2,1)}, u32[]{:S(2)}, u32[]{:S(2)}) collective-permute-start(bf16[2,2,2,2,32,4096]{5,4,3,2,1,0:T(8,128)(2,1)} %convolution_convert_fusion), channel_id=1, source_target_pairs={{0,2},{2,0},{4,6},{6,4},{8,10},{10,8},{12,14},{14,12},{16,18},{18,... | collective-permute-start | bytes 12582920 | tf_op jit(solution)/shard_map/ppermute | solution.py:52
  190.9 112.8 %collective-permute-start.19 = (bf16[2,2,2,2,128,1024]{5,4,3,2,1,0:T(8,128)(2,1)}, bf16[2,2,2,2,128,1024]{5,4,3,2,1,0:T(8,128)(2,1)}, u32[]{:S(2)}, u32[]{:S(2)}) collective-permute-start(bf16[2,2,2,2,128,1024]{5,4,3,2,1,0:T(8,128)(2,1)} %convolution_convert_fusion.2), channel_id=1, source_target_pairs={{0,2},{2,0},{4,6},{6,4},{8,10},{10,8},{12,14},{14,12},{16,18},{18,... | collective-permute-start | bytes 12582920 | tf_op jit(solution)/shard_map/ppermute | solution.py:52
  217.2 22.3 %slice-start = ((s8[13107200]{0:T(1024)(128)(4,1)}), s8[524288]{0:T(1024)(128)(4,1)S(1)}, s32[]{:S(2)}) async-start(s8[13107200]{0:T(1024)(128)(4,1)} %bitcast.466), calls=%async_computation | async-start | bytes 1048576
  220.9 18.6 %slice-start.1 = ((s8[13107200]{0:T(1024)(128)(4,1)}), s8[4194304]{0:T(1024)(128)(4,1)S(1)}, s32[]{:S(2)}) async-start(s8[13107200]{0:T(1024)(128)(4,1)} %bitcast.466), calls=%async_computation.1 | async-start | bytes 8388608
  220.9 18.6 %slice-start.2 = ((s8[13107200]{0:T(1024)(128)(4,1)}), s8[4194304]{0:T(1024)(128)(4,1)S(1)}, s32[]{:S(2)}) async-start(s8[13107200]{0:T(1024)(128)(4,1)} %bitcast.466), calls=%async_computation.2 | async-start | bytes 8388608
  221.0 18.6 %slice-start.3 = ((s8[13107200]{0:T(1024)(128)(4,1)}), s8[4194304]{0:T(1024)(128)(4,1)S(1)}, s32[]{:S(2)}) async-start(s8[13107200]{0:T(1024)(128)(4,1)} %bitcast.466), calls=%async_computation.3 | async-start | bytes 8388608
  234.1 27.9 %collective-permute-start.8 = (bf16[2,2,2,32,2240]{4,3,0,2,1:T(8,128)(2,1)S(1)}, bf16[2,2,2,32,2240]{4,3,0,2,1:T(8,128)(2,1)S(1)}, u32[]{:S(2)}, u32[]{:S(2)}) collective-permute-start(bf16[2,2,2,32,2240]{4,3,0,2,1:T(8,128)(2,1)S(1)} %fusion.25), channel_id=1, source_target_pairs={{0,1},{1,0},{2,3},{3,2},{4,5},{5,4},{6,7},{7,6},{8,9},{9,8},{10,11... | collective-permute-start | bytes 3440648 | tf_op jit(solution)/shard_map/ppermute | solution.py:52
  242.0 80.5 %collective-permute-start.3 = (bf16[2,2,2,32,3200]{4,3,0,2,1:T(8,128)(2,1)S(1)}, bf16[2,2,2,32,3200]{4,3,0,2,1:T(8,128)(2,1)S(1)}, u32[]{:S(2)}, u32[]{:S(2)}) collective-permute-start(bf16[2,2,2,32,3200]{4,3,0,2,1:T(8,128)(2,1)S(1)} %fusion.14), channel_id=1, source_target_pairs={{0,4},{2,6},{4,0},{6,2},{8,12},{10,14},{12,8},{14,10},{16,20},{18,... | collective-permute-start | bytes 4915208 | tf_op jit(solution)/shard_map/ppermute | solution.py:52
  262.2 30.0 %collective-permute-start.9 = (bf16[2,2,32,2240]{3,2,1,0:T(8,128)(2,1)S(1)}, bf16[2,2,32,2240]{3,2,1,0:T(8,128)(2,1)S(1)}, u32[]{:S(2)}, u32[]{:S(2)}) collective-permute-start(bf16[2,2,32,2240]{3,2,1,0:T(8,128)(2,1)S(1)} %fusion.86), channel_id=1, source_target_pairs={{0,4},{2,6},{4,0},{6,2},{8,12},{10,14},{12,8},{14,10},{16,20},{18,... | collective-permute-start | bytes 1720328 | tf_op jit(solution)/shard_map/ppermute | solution.py:52
  292.3 20.8 %collective-permute-start.10 = (bf16[2,32,2240]{2,1,0:T(8,128)(2,1)S(1)}, bf16[2,32,2240]{2,1,0:T(8,128)(2,1)S(1)}, u32[]{:S(2)}, u32[]{:S(2)}) collective-permute-start(bf16[2,32,2240]{2,1,0:T(8,128)(2,1)S(1)} %get-tuple-element.94), channel_id=1, source_target_pairs={{0,8},{2,10},{4,12},{6,14},{8,0},{10,2},{12,4},{14,6},{16,24},{18,... | collective-permute-start | bytes 860168 | tf_op jit(solution)/shard_map/ppermute | solution.py:52
  297.0 26.7 %collective-permute-start.13 = (bf16[2,2,2,32,2048]{4,3,2,1,0:T(8,128)(2,1)S(1)}, bf16[2,2,2,32,2048]{4,3,2,1,0:T(8,128)(2,1)S(1)}, u32[]{:S(2)}, u32[]{:S(2)}) collective-permute-start(bf16[2,2,2,32,2048]{4,3,2,1,0:T(8,128)(2,1)S(1)} %add_convert_fusion.6), channel_id=1, source_target_pairs={{0,1},{1,0},{2,3},{3,2},{4,5},{5,4},{6,7},{7,6},{8,9},{9,8},{10,11... | collective-permute-start | bytes 3145736 | tf_op jit(solution)/shard_map/ppermute | solution.py:52
  301.0 26.2 %collective-permute-start.14 = (bf16[2,2,2,32,2048]{4,3,2,1,0:T(8,128)(2,1)S(1)}, bf16[2,2,2,32,2048]{4,3,2,1,0:T(8,128)(2,1)S(1)}, u32[]{:S(2)}, u32[]{:S(2)}) collective-permute-start(bf16[2,2,2,32,2048]{4,3,2,1,0:T(8,128)(2,1)S(1)} %add_convert_fusion.4), channel_id=1, source_target_pairs={{0,4},{2,6},{4,0},{6,2},{8,12},{10,14},{12,8},{14,10},{16,20},{18,... | collective-permute-start | bytes 3145736 | tf_op jit(solution)/shard_map/ppermute | solution.py:52
  307.3 38.3 %collective-permute-start.20 = (bf16[2,2,2,128,512]{4,3,2,1,0:T(8,128)(2,1)S(1)}, bf16[2,2,2,128,512]{4,3,2,1,0:T(8,128)(2,1)S(1)}, u32[]{:S(2)}, u32[]{:S(2)}) collective-permute-start(bf16[2,2,2,128,512]{4,3,2,1,0:T(8,128)(2,1)S(1)} %add_convert_fusion.2), channel_id=1, source_target_pairs={{0,1},{1,0},{2,3},{3,2},{4,5},{5,4},{6,7},{7,6},{8,9},{9,8},{10,11... | collective-permute-start | bytes 3145736 | tf_op jit(solution)/shard_map/ppermute | solution.py:52
  313.2 7.7 %collective-permute-start.11 = (bf16[32,2240]{1,0:T(8,128)(2,1)S(1)}, bf16[32,2240]{1,0:T(8,128)(2,1)S(1)}, u32[]{:S(2)}, u32[]{:S(2)}) collective-permute-start(bf16[32,2240]{1,0:T(8,128)(2,1)S(1)} %fusion.169), channel_id=1, source_target_pairs={{0,16},{2,18},{4,20},{6,22},{8,24},{10,26},{12,28},{14,30},{16,0},... | collective-permute-start | bytes 430088 | tf_op jit(solution)/shard_map/ppermute | solution.py:52
  320.9 28.7 %collective-permute-start.21 = (bf16[2,2,2,128,512]{4,3,2,1,0:T(8,128)(2,1)S(1)}, bf16[2,2,2,128,512]{4,3,2,1,0:T(8,128)(2,1)S(1)}, u32[]{:S(2)}, u32[]{:S(2)}) collective-permute-start(bf16[2,2,2,128,512]{4,3,2,1,0:T(8,128)(2,1)S(1)} %add_convert_fusion), channel_id=1, source_target_pairs={{0,4},{2,6},{4,0},{6,2},{8,12},{10,14},{12,8},{14,10},{16,20},{18,... | collective-permute-start | bytes 3145736 | tf_op jit(solution)/shard_map/ppermute | solution.py:52
  322.8 40.4 %collective-permute-start.4 = (bf16[2,2,32,3200]{3,2,1,0:T(8,128)(2,1)S(1)}, bf16[2,2,32,3200]{3,2,1,0:T(8,128)(2,1)S(1)}, u32[]{:S(2)}, u32[]{:S(2)}) collective-permute-start(bf16[2,2,32,3200]{3,2,1,0:T(8,128)(2,1)S(1)} %fusion.83), channel_id=1, source_target_pairs={{0,1},{1,0},{2,3},{3,2},{4,5},{5,4},{6,7},{7,6},{8,9},{9,8},{10,11... | collective-permute-start | bytes 2457608 | tf_op jit(solution)/shard_map/ppermute | solution.py:52
  324.1 40.4 %collective-permute-start.15 = (bf16[2,2,32,2048]{3,2,1,0:T(8,128)(2,1)S(1)}, bf16[2,2,32,2048]{3,2,1,0:T(8,128)(2,1)S(1)}, u32[]{:S(2)}, u32[]{:S(2)}) collective-permute-start(bf16[2,2,32,2048]{3,2,1,0:T(8,128)(2,1)S(1)} %get-tuple-element.89), channel_id=1, source_target_pairs={{0,4},{2,6},{4,0},{6,2},{8,12},{10,14},{12,8},{14,10},{16,20},{18,... | collective-permute-start | bytes 1572872 | tf_op jit(solution)/shard_map/ppermute | solution.py:52
  327.8 46.6 %collective-permute-start.16 = (bf16[2,2,32,2048]{3,2,1,0:T(8,128)(2,1)S(1)}, bf16[2,2,32,2048]{3,2,1,0:T(8,128)(2,1)S(1)}, u32[]{:S(2)}, u32[]{:S(2)}) collective-permute-start(bf16[2,2,32,2048]{3,2,1,0:T(8,128)(2,1)S(1)} %get-tuple-element.87), channel_id=1, source_target_pairs={{0,1},{1,0},{2,3},{3,2},{4,5},{5,4},{6,7},{7,6},{8,9},{9,8},{10,11... | collective-permute-start | bytes 1572872 | tf_op jit(solution)/shard_map/ppermute | solution.py:52
  346.0 29.7 %collective-permute-start.22 = (bf16[2,2,128,512]{3,2,1,0:T(8,128)(2,1)S(1)}, bf16[2,2,128,512]{3,2,1,0:T(8,128)(2,1)S(1)}, u32[]{:S(2)}, u32[]{:S(2)}) collective-permute-start(bf16[2,2,128,512]{3,2,1,0:T(8,128)(2,1)S(1)} %get-tuple-element.85), channel_id=1, source_target_pairs={{0,4},{2,6},{4,0},{6,2},{8,12},{10,14},{12,8},{14,10},{16,20},{18,... | collective-permute-start | bytes 1572872 | tf_op jit(solution)/shard_map/ppermute | solution.py:52
  350.0 33.2 %collective-permute-start.23 = (bf16[2,2,128,512]{3,2,1,0:T(8,128)(2,1)S(1)}, bf16[2,2,128,512]{3,2,1,0:T(8,128)(2,1)S(1)}, u32[]{:S(2)}, u32[]{:S(2)}) collective-permute-start(bf16[2,2,128,512]{3,2,1,0:T(8,128)(2,1)S(1)} %get-tuple-element.83), channel_id=1, source_target_pairs={{0,1},{1,0},{2,3},{3,2},{4,5},{5,4},{6,7},{7,6},{8,9},{9,8},{10,11... | collective-permute-start | bytes 1572872 | tf_op jit(solution)/shard_map/ppermute | solution.py:52
  363.4 21.6 %collective-permute-start.5 = (bf16[2,32,3200]{2,1,0:T(8,128)(2,1)S(1)}, bf16[2,32,3200]{2,1,0:T(8,128)(2,1)S(1)}, u32[]{:S(2)}, u32[]{:S(2)}) collective-permute-start(bf16[2,32,3200]{2,1,0:T(8,128)(2,1)S(1)} %get-tuple-element.92), channel_id=1, source_target_pairs={{0,8},{2,10},{4,12},{6,14},{8,0},{10,2},{12,4},{14,6},{16,24},{18,... | collective-permute-start | bytes 1228808 | tf_op jit(solution)/shard_map/ppermute | solution.py:52
  374.6 12.6 %collective-permute-start.17 = (bf16[2,2,32,2048]{3,2,0,1:T(8,128)(2,1)S(1)}, bf16[2,2,32,2048]{3,2,0,1:T(8,128)(2,1)S(1)}, u32[]{:S(2)}, u32[]{:S(2)}) collective-permute-start(bf16[2,2,32,2048]{3,2,0,1:T(8,128)(2,1)S(1)} %fusion.93), channel_id=1, source_target_pairs={{0,8},{2,10},{4,12},{6,14},{8,0},{10,2},{12,4},{14,6},{16,24},{18,... | collective-permute-start | bytes 1572872 | tf_op jit(solution)/shard_map/ppermute | solution.py:52
  383.4 21.7 %collective-permute-start.24 = (bf16[2,2,128,512]{3,2,0,1:T(8,128)(2,1)S(1)}, bf16[2,2,128,512]{3,2,0,1:T(8,128)(2,1)S(1)}, u32[]{:S(2)}, u32[]{:S(2)}) collective-permute-start(bf16[2,2,128,512]{3,2,0,1:T(8,128)(2,1)S(1)} %fusion.94), channel_id=1, source_target_pairs={{0,8},{2,10},{4,12},{6,14},{8,0},{10,2},{12,4},{14,6},{16,24},{18,... | collective-permute-start | bytes 1572872 | tf_op jit(solution)/shard_map/ppermute | solution.py:52
  385.1 20.8 %collective-permute-start.6 = (bf16[32,3200]{1,0:T(8,128)(2,1)S(1)}, bf16[32,3200]{1,0:T(8,128)(2,1)S(1)}, u32[]{:S(2)}, u32[]{:S(2)}) collective-permute-start(bf16[32,3200]{1,0:T(8,128)(2,1)S(1)} %fusion.167), channel_id=1, source_target_pairs={{0,16},{2,18},{4,20},{6,22},{8,24},{10,26},{12,28},{14,30},{16,0},... | collective-permute-start | bytes 614408 | tf_op jit(solution)/shard_map/ppermute | solution.py:52
  388.0 24.5 %collective-permute-start.18 = (bf16[2,32,2048]{2,1,0:T(8,128)(2,1)}, bf16[2,32,2048]{2,1,0:T(8,128)(2,1)S(1)}, u32[]{:S(2)}, u32[]{:S(2)}) collective-permute-start(bf16[2,32,2048]{2,1,0:T(8,128)(2,1)} %fusion.131), channel_id=1, source_target_pairs={{0,16},{2,18},{4,20},{6,22},{8,24},{10,26},{12,28},{14,30},{16,0},... | collective-permute-start | bytes 786440 | tf_op jit(solution)/shard_map/ppermute | solution.py:52
  405.1 12.9 %collective-permute-start.25 = (bf16[2,128,512]{2,1,0:T(8,128)(2,1)S(1)}, bf16[2,128,512]{2,1,0:T(8,128)(2,1)S(1)}, u32[]{:S(2)}, u32[]{:S(2)}) collective-permute-start(bf16[2,128,512]{2,1,0:T(8,128)(2,1)S(1)} %fusion.133), channel_id=1, source_target_pairs={{0,16},{2,18},{4,20},{6,22},{8,24},{10,26},{12,28},{14,30},{16,0},... | collective-permute-start | bytes 786440 | tf_op jit(solution)/shard_map/ppermute | solution.py:52
  (49 other events, 215.6 us)

commit v2 on v1

--- a/solution.py
+++ b/solution.py
@@ -1,8 +1,11 @@
+import functools
 import math
 
 import jax
 import jax.numpy as jnp
 from jax import lax
+from jax.experimental import pallas as pl
+from jax.experimental.pallas import tpu as pltpu
 from jax.sharding import PartitionSpec as P
 
 HEADS = 4
@@ -10,6 +13,7 @@
 EXPERTS = 5
 
 eps = 1e-06
+VMEM = 56 << 20
 
 
 def product(left, right):
@@ -36,46 +40,167 @@
 
 class Grid:
     def __init__(self):
-        self.sizes = {"seq": lax.axis_size("seq"), "batch": lax.axis_size("batch")}
-        self.bits = []
-        for axis in ("seq", "batch"):
-            count = self.sizes[axis].bit_length() - 1
-            self.bits += [(axis, at) for at in reversed(range(count))]
-        self.index = {"seq": lax.axis_index("seq"), "batch": lax.axis_index("batch")}
-
-    def mine(self, bit):
-        axis, at = bit
-        return (self.index[axis] >> at) & 1
-
-    def swap(self, value, bit):
-        axis, at = bit
-        return lax.ppermute(
-            value, axis, [(i, i ^ (1 << at)) for i in range(self.sizes[axis])]
-        )
-
-
-class Shards:
-    def __init__(self, array, bits):
-        self.array, self.bits = array, list(bits)
-
-    def pick(self, bit, value):
-        at = self.bits.index(bit)
-        rest = self.bits[:at] + self.bits[at + 1 :]
-        return Shards(lax.dynamic_index_in_dim(self.array, value, at, keepdims=False), rest)
-
-    def map(self, f):
-        return Shards(f(self.array), self.bits)
-
-
-def flat_rows(array, tail):
-    return array.reshape((-1,) + array.shape[array.ndim - tail :])
-
-
-def reduce_pair(grid, parts, bit):
-    mine = grid.mine(bit)
-    sent = parts(1 - mine).map(lambda a: a.astype(jnp.bfloat16))
-    came = Shards(grid.swap(sent.array, bit), sent.bits)
-    return came, (lambda: parts(mine))
+        self.seq, self.batch = lax.axis_size("seq"), lax.axis_size("batch")
+        self.count = self.seq * self.batch
+        low = self.batch.bit_length() - 1
+        self.core, self.plane_a, self.plane_b = 1 << low, 1, 2 << low
+        taken = self.core | self.plane_a | self.plane_b
+        masks = [m for m in range(self.count) if not m & taken]
+        self.rest = masks
+        self.me = lax.axis_index("seq") * self.batch + lax.axis_index("batch")
+
+    def swap(self, value, mask):
+        both = ("seq", "batch")
+        return lax.ppermute(value, both, [(i, i ^ mask) for i in range(self.count)])
+
+    def order(self, first, second, theirs):
+        base = self.core if theirs else 0
+        masks = [
+            base | f | s | m for f in (first, 0) for s in (second, 0) for m in self.rest
+        ]
+        return self.me ^ jnp.array(masks, jnp.int32)
+
+
+def after(value, *others):
+    return lax.optimization_barrier((value,) + others)[0]
+
+
+def rows_kernel(adding, src_ref, left_ref, right_ref, *refs):
+    turned = refs[-1]
+    order, at = pl.program_id(0), pl.program_id(1)
+
+    @pl.when(at == 0)
+    def _():
+        places = lax.broadcasted_iota(jnp.int32, (turned.shape[0], left_ref.shape[1]), 1)
+        picks = (src_ref[0] == places).astype(jnp.float32).astype(jnp.bfloat16)
+        turned[...] = product_nt(picks, left_ref[...]).astype(jnp.bfloat16)
+
+    total = product(turned[...], right_ref[...])
+    if not adding:
+        refs[0][0] = total.astype(jnp.bfloat16)
+        return
+    total = (total + refs[0][0].astype(jnp.float32)).astype(jnp.bfloat16)
+    half = total.shape[0] // 2
+    for number in range(2):
+
+        @pl.when(order == number)
+        def _():
+            refs[1 + 2 * number][...] = total[:half]
+            refs[2 + 2 * number][...] = total[half:]
+
+
+def gradient_rows(src, left, right, steps, came=None):
+    tokens, features = left.shape
+    columns = right.shape[1] // 2
+    size = columns // steps
+    rows = src.shape[1]
+    in_specs = [
+        pl.BlockSpec((1, rows, 1), lambda o, j: (o, 0, 0)),
+        pl.BlockSpec((tokens, features), lambda o, j: (0, 0)),
+        pl.BlockSpec((tokens, size), lambda o, j: (0, o * steps + j)),
+    ]
+    operands = [src, left, right]
+    paired = pl.BlockSpec((1, rows, size), lambda o, j: (o, 0, j))
+    if came is None:
+        out_shape = jax.ShapeDtypeStruct((2, rows, columns), jnp.bfloat16)
+        out_specs = paired
+    else:
+        in_specs.append(paired)
+        operands.append(came)
+        out_shape = [jax.ShapeDtypeStruct((rows // 2, columns), jnp.bfloat16)] * 4
+        early = pl.BlockSpec((rows // 2, size), lambda o, j: (0, jnp.where(o == 0, j, steps - 1)))
+        late = pl.BlockSpec((rows // 2, size), lambda o, j: (0, jnp.where(o == 0, 0, j)))
+        out_specs = [early, early, late, late]
+    return pl.pallas_call(
+        functools.partial(rows_kernel, came is not None),
+        grid=(2, steps),
+        in_specs=in_specs,
+        out_specs=out_specs,
+        out_shape=out_shape,
+        scratch_shapes=[pltpu.VMEM((rows, tokens), jnp.bfloat16)],
+        compiler_params=pltpu.CompilerParams(vmem_limit_bytes=VMEM),
+        cost_estimate=pl.CostEstimate(
+            flops=4 * rows * tokens * columns,
+            bytes_accessed=2 * (tokens * features + 2 * columns * (tokens + rows)),
+            transcendentals=0,
+        ),
+    )(*operands)
+
+
+def units_kernel(adding, order_ref, left_ref, right_ref, *refs):
+    order, at = pl.program_id(0), pl.program_id(1)
+    blocks = order_ref.shape[1] // 2
+    chosen = jnp.concatenate(
+        [
+            left_ref[:, pl.ds(pl.multiple_of(order_ref[order, at * blocks + i] * 128, 128), 128)]
+            for i in range(blocks)
+        ],
+        1,
+    )
+    total = product_tn(chosen, right_ref[...])
+    if not adding:
+        refs[0][0] = total.astype(jnp.bfloat16)
+        return
+    total = (total + refs[0][0].astype(jnp.float32)).astype(jnp.bfloat16)
+    for number in range(4):
+
+        @pl.when(order * 2 + at == number)
+        def _():
+            refs[1 + number][...] = total
+
+
+def gradient_units(order, left, right, came=None):
+    tokens = left.shape[0]
+    rows, columns = order.shape[1] * 128, right.shape[1] // 2
+    paired = pl.BlockSpec((1, rows // 2, columns), lambda o, j, *_: (o, j, 0))
+    in_specs = [
+        pl.BlockSpec(left.shape, lambda o, j, *_: (0, 0)),
+        pl.BlockSpec((tokens, columns), lambda o, j, *_: (0, o)),
+    ]
+    operands = [order, left, right]
+    if came is None:
+        out_shape = jax.ShapeDtypeStruct((2, rows, columns), jnp.bfloat16)
+        out_specs = paired
+    else:
+        in_specs.append(paired)
+        operands.append(came)
+        out_shape = [jax.ShapeDtypeStruct((rows // 2, columns), jnp.bfloat16)] * 4
+        out_specs = [pl.BlockSpec((rows // 2, columns), lambda o, j, *_: (0, 0))] * 4
+    return pl.pallas_call(
+        functools.partial(units_kernel, came is not None),
+        grid_spec=pltpu.PrefetchScalarGridSpec(
+            num_scalar_prefetch=1, grid=(2, 2), in_specs=in_specs, out_specs=out_specs
+        ),
+        out_shape=out_shape,
+        compiler_params=pltpu.CompilerParams(vmem_limit_bytes=VMEM),
+        cost_estimate=pl.CostEstimate(
+            flops=4 * rows * tokens * columns,
+            bytes_accessed=2 * (left.size + right.size + 4 * rows * columns),
+            transcendentals=0,
+        ),
+    )(*operands)
+
+
+def added(kept, came, pieces):
+    size = kept.shape[0] // pieces
+    return [
+        kept[i * size : (i + 1) * size].astype(jnp.float32)
+        + came[i * size : (i + 1) * size].astype(jnp.float32)
+        for i in range(pieces)
+    ]
+
+
+def second_halving(grid, kept, came, mask):
+    sent, own = (part.astype(jnp.bfloat16) for part in added(kept, came, 2))
+    return own, grid.swap(sent, mask)
+
+
+def last_sum(grid, kept, came):
+    parts = added(kept, came, len(grid.rest))
+    total = parts[0]
+    for part, mask in zip(parts[1:], grid.rest[1:]):
+        total = total + grid.swap(part.astype(jnp.bfloat16), mask).astype(jnp.float32)
+    return total
 
 
 def norm_forward(field, gain):
@@ -180,10 +305,15 @@
     cotangent,
 ):
     grid = Grid()
-    bits = grid.bits
-    cube = (2,) * len(bits)
-    core, plane_a, plane_b = ("seq", 0), ("batch", 0), ("seq", 1)
-    rest = [b for b in reversed(bits) if b not in (core, plane_a, plane_b)]
+    orders = [
+        jnp.stack(
+            [
+                grid.order(grid.plane_a, grid.plane_b, theirs),
+                grid.order(grid.plane_b, grid.plane_a, theirs),
+            ]
+        )
+        for theirs in (True, False)
+    ]
     micro, _, block, width = tokens.shape
     rows = micro * block
     hidden_units = w_up.shape[1]
@@ -252,25 +382,40 @@
     d_down = cotangent.reshape(rows, width)
     grad_out = d_down.astype(jnp.float32)
 
-    upper_t = Shards(upper.T.reshape(cube + (-1, rows)), bits)
-    staged_down = core_stage(grid, upper_t, d_down)
-    d_pre = (product_nt(d_down, w_down) * slope).astype(jnp.bfloat16)
-    normed_two_t = Shards(normed_two.T.reshape(cube + (-1, rows)), bits)
-    staged_up = core_stage(grid, normed_two_t, d_pre)
-    half = width // 2
-    down_a = plane_stage(grid, staged_down, plane_a, plane_b, slice(0, half))
-    down_b = plane_stage(grid, staged_down, plane_b, plane_a, slice(half, width))
-    half = hidden_units // 2
-    up_a = plane_stage(grid, staged_up, plane_a, plane_b, slice(0, half))
-    up_b = plane_stage(grid, staged_up, plane_b, plane_a, slice(half, hidden_units))
+    share = width // grid.count
+    sources = [
+        (order[:, :, None] * share + jnp.arange(share, dtype=jnp.int32)).reshape(2, -1, 1)
+        for order in orders
+    ]
+    units = hidden_units // grid.count
+    if units == 128:
+        unit_left, unit_orders = [upper, upper], orders
+    else:
+        lists = [(o[:, :, None] * units + jnp.arange(units)).reshape(-1) for o in orders]
+        unit_left = [upper[:, at] for at in lists]
+        unit_orders = [jnp.arange(hidden_units // 128, dtype=jnp.int32).reshape(2, -1)] * 2
+    down_sent = gradient_units(unit_orders[0], unit_left[0], d_down)
+    down_came = grid.swap(down_sent, grid.core)
+    d_up = after(d_down, down_sent)
+    d_pre = (product_nt(d_up, w_down) * slope).astype(jnp.bfloat16)
+    up_sent = gradient_rows(sources[0], normed_two, d_pre, 2)
+    up_came = grid.swap(up_sent, grid.core)
+    down_parts = gradient_units(unit_orders[1], unit_left[1], after(d_down, up_sent), down_came)
+    down_one = [grid.swap(down_parts[0], grid.plane_a), grid.swap(down_parts[2], grid.plane_b)]
+    up_parts = gradient_rows(sources[1], after(normed_two, *down_parts), d_pre, 2, up_came)
+    up_one = [grid.swap(up_parts[0], grid.plane_a), grid.swap(up_parts[2], grid.plane_b)]
+    d_pre = after(d_pre, *up_parts)
     d_normed_two = product_nt(d_pre, w_up)
     d_hidden_norm, grad_gain_two = norm_backward(hidden, factor_two, gain_two, d_normed_two)
     d_hidden = grad_out + d_hidden_norm
     d_branch = d_hidden.astype(jnp.bfloat16)
-    branch_t = Shards(d_branch.T.reshape(cube + (-1, rows)), bits)
-    staged_out = core_stage(grid, branch_t, mixed)
-    d_mixed = product_nt(d_branch, w_out).reshape(rows, HEADS, EXPERTS, HEAD)
-    out_pair = plane_stage(grid, staged_out, plane_a, plane_b, slice(0, mixed.shape[1]))
+    mixed_wide = jnp.pad(mixed, ((0, 0), (0, -mixed.shape[1] % 256)))
+    out_sent = gradient_rows(sources[0], d_branch, mixed_wide, 1)
+    out_came = grid.swap(out_sent, grid.core)
+    d_mixed = product_nt(after(d_branch, out_sent), w_out)
+    out_parts = gradient_rows(sources[1], after(d_branch, d_mixed), mixed_wide, 1, out_came)
+    out_one = [grid.swap(out_parts[0], grid.plane_a), grid.swap(out_parts[2], grid.plane_b)]
+    d_mixed = after(d_mixed, *out_parts).reshape(rows, HEADS, EXPERTS, HEAD)
     result = (hidden + product(upper, w_down)).astype(jnp.bfloat16)
     d_attended = jnp.sum(out_gates[..., None] * d_mixed, axis=2).astype(jnp.bfloat16)
     d_ogate = jnp.sum(attended_f[:, :, None, :] * d_mixed, axis=3)
@@ -338,39 +483,65 @@
     d_field_norm, grad_gain_one = norm_backward(field, factor_one, gain_one, d_normed)
     field_grad = (d_hidden + d_field_norm).astype(jnp.bfloat16)
 
-    wide = jnp.concatenate([d_query, d_keys, d_expert, d_vlogit, d_ologit], 1)
-    used = wide.shape[1]
-    full = -(-(used + 2) // 128) * 128
-    wide = jnp.pad(wide, ((0, 0), (0, full - used)))
-    gains = jnp.stack([grad_gain_one, grad_gain_two], 1)
-    gains = jnp.pad(gains, ((0, 0), (used, full - used - 2)))
-    gains = Shards(gains.reshape(cube + (-1, full)), bits)
-    normed_t = Shards(normed.T.reshape(cube + (-1, rows)), bits)
-    staged_in = core_stage(grid, normed_t, wide, gains)
-    in_pair = plane_stage(grid, staged_in, plane_b, plane_a, slice(0, full))
-
-    down = rest_stages(grid, joined([down_a, down_b]), rest)
-    grad_down = jnp.concatenate([down[0], down[1]], -1)
-    up = rest_stages(grid, joined([up_a, up_b]), rest)
-    grad_up = jnp.concatenate([up[0], up[1]], -1)
-    grad_out_w = rest_stages(grid, out_pair, rest).T
-    grad_in = rest_stages(grid, in_pair, rest)
-    pieces = []
-    start = 0
-    for size in (w_query.shape[1], w_key.shape[1], w_value.shape[1], w_vgate.shape[1], w_ogate.shape[1]):
-        pieces.append(grad_in[:, start : start + size])
-        start += size
+    pads, starts, total = [], [], 0
+    for piece in (d_expert, d_query, d_keys, jnp.concatenate([d_vlogit, d_ologit], 1)):
+        starts.append(total)
+        pads.append(jnp.pad(piece, ((0, 0), (0, -piece.shape[1] % 128))))
+        total += pads[-1].shape[1]
+    gates = d_vlogit.shape[1]
+    spare = starts[3] + 2 * gates
+    more = -total % 256
+    pads[-1] = jnp.pad(pads[-1], ((0, 0), (0, more)))
+    total += more
+    extra_left, extra_right = [], []
+    for number, gain in enumerate((grad_gain_one, grad_gain_two)):
+        for _ in range(3):
+            low = gain.astype(jnp.bfloat16)
+            gain = gain - low.astype(jnp.float32)
+            extra_left.append(low)
+            extra_right.append(jnp.arange(total) == spare + number)
+    fill = 16 - len(extra_left)
+    left = jnp.concatenate([normed, jnp.pad(jnp.stack(extra_left), ((0, fill), (0, 0)))], 0)
+    right = jnp.concatenate(
+        [
+            jnp.concatenate(pads, 1),
+            jnp.pad(jnp.stack(extra_right).astype(jnp.bfloat16), ((0, fill), (0, 0))),
+        ],
+        0,
+    )
+    in_sent = gradient_rows(sources[0], left, right, 1)
+    in_came = grid.swap(in_sent, grid.core)
+    in_parts = gradient_rows(sources[1], left, right, 1, in_came)
+    in_one = [grid.swap(in_parts[0], grid.plane_a), grid.swap(in_parts[2], grid.plane_b)]
+
+    def finished(parts, one):
+        first = second_halving(grid, parts[1], one[0], grid.plane_b)
+        second = second_halving(grid, parts[3], one[1], grid.plane_a)
+        kept, came = (jnp.concatenate(pair, 1) for pair in zip(first, second))
+        return last_sum(grid, kept, came)
+
+    grad_down = finished(down_parts, down_one)
+    grad_up = finished(up_parts, up_one)
+    grad_out_w = finished(out_parts, out_one)[:, : mixed.shape[1]].T
+    grad_in = finished(in_parts, in_one)
+    pieces = [
+        grad_in[:, starts[1] : starts[1] + w_query.shape[1]],
+        grad_in[:, starts[2] : starts[2] + w_key.shape[1]],
+        grad_in[:, : w_value.shape[1]],
+        grad_in[:, starts[3] : starts[3] + gates],
+        grad_in[:, starts[3] + gates : spare],
+    ]
     return (
         result.reshape(tokens.shape),
         field_grad.reshape(tokens.shape),
-        grad_in[:, start],
+        grad_in[:, spare],
         pieces[0],
         pieces[1],
         pieces[2],
         pieces[3],
         pieces[4],
         grad_out_w,
-        grad_in[:, start + 1],
+        grad_in[:, spare + 1],
         grad_up,
         grad_down,
     )

time: 426 us -> 420 us (0.986)
  the two profiles are of different devices: /device:TPU:0 before, /device:TPU:8 now
where the time goes in v2:
time: 420 us; the launch traced here: 412 us
  waiting for transfers between devices  89.8 us (21%)
  matrix products  89.7 us (21%)
  Pallas kernels  68.1 us (16%)
  other arithmetic  63.1 us (15%)
  local copies, waits for them, and re-layouts  58.9 us (14%)
  starting transfers between devices  40.4 us (10%)
    ppermute x32, waiting for transfers between devices, swap(): return lax.ppermute(value, both, [(i, i ^ mask) for i in range(self.count)])  89.8 us
    pallas_call x6, Pallas kernels, gradient_rows(): pl.pallas_call(functools.partial(rows_kernel, came is not None), grid=(2,...  50.8 us
    dot_general x8, matrix products, product_nt(): lax.dot_general(left, right, (((1,), (1,)), ((), ())), preferred_element_...  50.2 us
    ppermute x32, starting transfers between devices, swap(): return lax.ppermute(value, both, [(i, i ^ mask) for i in range(self.count)])  34.8 us
    dot_general x8, matrix products, product(): return jnp.dot(left, right, preferred_element_type=jnp.float32)  32.3 us
    pallas_call x2, Pallas kernels, gradient_units(): pl.pallas_call(functools.partial(units_kernel, came is not None), grid_sp...  17.3 us
    unnamed x144, local copies, waits for them, and re-layouts  13.6 us
    convert_element_type x8, other arithmetic, second_halving(): sent, own = (part.astype(jnp.bfloat16) for part in added(kept, came, 2))  9.7 us
  transfers between devices with their start and end apart: 34, of which 12 were waited for; matrix products, arithmetic and copies ran while one was open for 42% of the time, Pallas kernels for 15%

profile of v2, /device:TPU:8, one launch (start us, length us, event | category | flops | bytes accessed | tf_op | source)
XLA Modules:
  0.0 411.9 jit_solution(4683349602830144551)
XLA Ops:
  9.4 8.0 %multiply_reduce_fusion.3 = (bf16[512,4,112]{0,2,1:T(8,128)(2,1)}, f32[512,4,5,112]{0,3,2,1:T(8,128)}) fusion(f32[512,4,5]{0,2,1:T(8,128)S(1)} %copy.146, bf16[512,1024,1,1]{1,0,3,2:T(8,128)(2,1)S(1)} %bitcast.174, bf16[4,5,112,1024]{3,2,1,0:T(8,128)(2,1)} %bitcast.188), kind=kOutput, calls=%fused_computation.36 | convolution fusion | flops 2350874624 | bytes 10723328 | tf_op jit(solution)/shard_map/dot_general | solution.py:20
  17.4 3.7 collective-permute-start
  63.5 8.0 %multiply_convert_fusion = (bf16[512,4096]{1,0:T(8,128)(2,1)}, f32[512,4096]{1,0:T(8,128)}) fusion(bf16[512,1024]{1,0:T(8,128)(2,1)S(1)} %multiply_convert_fusion.4.left_ref, bf16[1024,4096]{1,0:T(8,128)(2,1)S(1)} %bitcast.185), kind=kOutput, calls=%fused_computation.12 | convolution fusion | flops 4305453056 | bytes 22020096 | tf_op jit(solution)/shard_map/dot_general | solution.py:20
  71.5 7.9 %shard_map.274 = bf16[2,2048,512]{2,1,0:T(8,128)(2,1)} custom-call(s32[2,16]{1,0:T(2,128)} %get-tuple-element.175.order_ref, bf16[512,4096]{1,0:T(8,128)(2,1)} %get-tuple-element.184.left_ref, bf16[512,1024]{1,0:T(8,128)(2,1)} %bitcast.155), custom_call_target="tpu_custom_call" | custom-call | flops 2147483648 | bytes 13631488 | tf_op jit(solution)/shard_map/pallas_call | solution.py:169
  79.4 11.5 %fusion.6.right_ref = bf16[512,4096]{1,0:T(8,128)(2,1)} fusion(f32[512,4096]{1,0:T(8,128)} %get-tuple-element.185, bf16[512,1024]{1,0:T(8,128)(2,1)S(1)} %bitcast.157, bf16[4096,1024]{1,0:T(8,128)(2,1)} %param.32), kind=kOutput, calls=%fused_computation.11 | convolution fusion | flops 4315938816 | bytes 22020096 | tf_op jit(solution)/shard_map/dot_general | solution.py:30
  90.9 8.1 %shard_map.275 = bf16[2,512,2048]{2,1,0:T(8,128)(2,1)} custom-call(s32[2,512,1]{2,1,0:T(8,128)} %get-tuple-element.170.src_ref, bf16[512,1024]{1,0:T(8,128)(2,1)} %copy-done.8, bf16[512,4096]{1,0:T(8,128)(2,1)} %fusion.6.right_ref), custom_call_target="tpu_custom_call" | custom-call | flops 2147483648 | bytes 9437184 | tf_op jit(solution)/shard_map/pallas_call | solution.py:114
  100.9 4.3 %copy.155 = bf16[512,2240]{1,0:T(8,128)(2,1)} copy(bf16[512,2240]{0,1:T(8,128)(2,1)} %bitcast.159) | data formatting | bytes 4587520 | tf_op jit(solution)/shard_map/convert_element_type | solution.py:374
  108.6 9.5 %add_convert_fusion = bf16[512,1024]{1,0:T(8,128)(2,1)} fusion(f32[512,1024]{1,0:T(8,128)} %copy-done.15, bf16[512,4096]{1,0:T(8,128)(2,1)S(1)} %copy-done.4, bf16[4096,1024]{1,0:T(8,128)(2,1)} %param.32), kind=kOutput, calls=%fused_computation.71 | convolution fusion | flops 4296015872 | bytes 15728640 | tf_op jit(solution)/shard_map/dot_general | solution.py:20
  118.1 9.4 %shard_map.276 = (bf16[1024,512]{1,0:T(8,128)(2,1)}, bf16[1024,512]{1,0:T(8,128)(2,1)}, bf16[1024,512]{1,0:T(8,128)(2,1)}, bf16[1024,512]{1,0:T(8,128)(2,1)}) custom-call(s32[2,16]{1,0:T(2,128)} %get-tuple-element.176.order_ref, bf16[512,4096]{1,0:T(8,128)(2,1)} %get-tuple-element.184.left_ref, bf16[512,1024]{1,0:T(8,128)(2,1)} %bitcast.156, ...), custom_call_target="tpu_custom_call" | custom-call | flops 2147483648 | bytes 13631488 | tf_op jit(solution)/shard_map/pallas_call | solution.py:169
  130.5 9.9 %shard_map.277 = (bf16[256,2048]{1,0:T(8,128)(2,1)}, bf16[256,2048]{1,0:T(8,128)(2,1)}, bf16[256,2048]{1,0:T(8,128)(2,1)}, bf16[256,2048]{1,0:T(8,128)(2,1)}) custom-call(s32[2,512,1]{2,1,0:T(8,128)} %get-tuple-element.171.src_ref, bf16[512,1024]{1,0:T(8,128)(2,1)} %copy-done.8, bf16[512,4096]{1,0:T(8,128)(2,1)} %fusion.6.right_ref, ...), custom_call_target="tpu_custom_call" | custom-call | flops 2147483648 | bytes 9437184 | tf_op jit(solution)/shard_map/pallas_call | solution.py:114
  141.4 8.9 %multiply_reduce_fusion.5 = (f32[1024]{0:T(1024)S(1)}, f32[512]{0:T(512)S(1)}, f32[512,1024]{1,0:T(8,128)S(1)}) fusion(f32[512,1024]{1,0:T(8,128)} %copy-done.15, f32[512]{0:T(512)S(1)} %get-tuple-element.169, f32[1024]{0:T(1024)S(1)} %convert_element_type.630, bf16[512,4096]{1,0:T(8,128)(2,1)S(1)} %copy-done.5, bf16[1024,4096]{1,0:T(8,128)(2,1)} %param.31), kind=kOutput, calls=%fused_computation.67 | convolution fusion | flops 4298111488 | bytes 16789504 | tf_op jit(solution)/shard_map/dot_general | solution.py:30
  152.7 6.3 %shard_map.278 = bf16[2,512,1152]{2,1,0:T(8,128)(2,1)} custom-call(s32[2,512,1]{2,1,0:T(8,128)} %get-tuple-element.170.src_ref, bf16[512,1024]{1,0:T(8,128)(2,1)} %get-tuple-element.48.left_ref, bf16[512,2304]{1,0:T(8,128)(2,1)} %pad.33.right_ref), custom_call_target="tpu_custom_call" | custom-call | flops 1207959552 | bytes 5767168 | tf_op jit(solution)/shard_map/pallas_call | solution.py:114
  159.2 7.1 %fusion.88 = f32[512,2240]{0,1:T(8,128)} fusion(bf16[512,1024]{1,0:T(8,128)(2,1)S(1)} %copy-done.11, bf16[2240,1024]{1,0:T(8,128)(2,1)} %param.29), kind=kOutput, calls=%fused_computation.249 | convolution fusion | flops 2348810240 | bytes 10223616 | tf_op jit(solution)/shard_map/dot_general | solution.py:30
  184.1 4.9 %collective-permute-done.29 = bf16[512,512]{1,0:T(8,128)(2,1)S(1)} collective-permute-done((bf16[512,512]{1,0:T(8,128)(2,1)S(1)}, bf16[512,512]{1,0:T(8,128)(2,1)S(1)}, u32[]{:S(2)}, u32[]{:S(2)}) %collective-permute-start.29) | collective-permute-done | bytes 524320 | tf_op jit(solution)/shard_map/ppermute | solution.py:54
  193.4 5.6 %collective-permute-done.22 = bf16[128,2048]{1,0:T(8,128)(2,1)S(1)} collective-permute-done((bf16[128,2048]{1,0:T(8,128)(2,1)S(1)}, bf16[128,2048]{1,0:T(8,128)(2,1)S(1)}, u32[]{:S(2)}, u32[]{:S(2)}) %collective-permute-start.22) | collective-permute-done | bytes 524320 | tf_op jit(solution)/shard_map/ppermute | solution.py:54
  203.7 7.2 %shard_map.279 = (bf16[256,1152]{1,0:T(8,128)(2,1)}, bf16[256,1152]{1,0:T(8,128)(2,1)}, bf16[256,1152]{1,0:T(8,128)(2,1)}, bf16[256,1152]{1,0:T(8,128)(2,1)}) custom-call(s32[2,512,1]{2,1,0:T(8,128)} %get-tuple-element.171.src_ref, bf16[512,1024]{1,0:T(8,128)(2,1)} %get-tuple-element.48.left_ref, bf16[512,2304]{1,0:T(8,128)(2,1)} %pad.33.right_ref, ...), custom_call_target="tpu_custom_call" | custom-call | flops 1207959552 | bytes 5767168 | tf_op jit(solution)/shard_map/pallas_call | solution.py:114
  211.0 3.8 multiply_reduce_fusion.2
  227.4 5.2 %multiply_convert_fusion.1 = (bf16[512,4,5,112]{0,3,2,1:T(8,128)(2,1)}, f32[512,4,5]{0,2,1:T(8,128)}) fusion(f32[512,4,112]{0,2,1:T(8,128)S(1)} %bitcast.169, f32[512,4,5]{0,2,1:T(8,128)S(1)} %copy-done.49, f32[512,4,5,112]{0,3,2,1:T(8,128)} %get-tuple-element.179), kind=kLoop, calls=%fused_computation.32 | loop fusion | flops 4577280 | bytes 7880704 | tf_op jit(solution)/shard_map/convert_element_type | solution.py:468
  232.5 4.6 %copy.166 = bf16[512,2240]{1,0:T(8,128)(2,1)} copy(bf16[512,2240]{0,1:T(8,128)(2,1)} %bitcast.160) | data formatting | bytes 4587520 | tf_op jit(solution)/shard_map/convert_element_type | solution.py:468
  237.2 6.9 %fusion.91 = f32[512,1024]{1,0:T(8,128)} fusion(bf16[512,2240]{0,1:T(8,128)(2,1)} %bitcast.161, bf16[1024,2240]{0,1:T(8,128)(2,1)} %param.26), kind=kOutput, calls=%fused_computation.252 | convolution fusion | flops 2348810240 | bytes 8978432 | tf_op jit(solution)/shard_map/dot_general | solution.py:30
  261.6 6.9 %fusion.38 = (f32[1024]{0:T(1024)S(1)}, f32[512]{0:T(512)}, f32[512,1024]{1,0:T(8,128)}) fusion(bf16[2,1,256,1024]{3,2,1,0:T(8,128)(2,1)S(1)} %copy-done.1, f32[512]{0:T(512)S(1)} %bitcast.178, f32[1024]{0:T(1024)S(1)} %convert_element_type.612, f32[512,1024]{1,0:T(8,128)} %fusion.92, f32[512,1024]{1,0:T(8,128)} %fusion.91, bf16[512,448]{0,1:T(8,128)(2,1)} %bitcast.168, ...), kind=kOutput, calls=%fused_computation.66 | convolution fusion | flops 475527680 | bytes 12922880 | tf_op jit(solution)/shard_map/dot_general | solution.py:30
  274.4 6.4 %fusion.22.right_ref = bf16[528,3584]{1,0:T(8,128)(2,1)} fusion(bf16[512,40]{1,0:T(8,128)(2,1)} %copy.169, bf16[512,448]{1,0:T(8,128)(2,1)} %copy.168, bf16[512,448]{1,0:T(8,128)(2,1)} %copy.167, bf16[512,2240]{1,0:T(8,128)(2,1)} %copy.166, bf16[16,3584]{1,0:T(8,128)(2,1)} %pad_convert_fusion), kind=kLoop, calls=%fused_computation.42 | loop fusion | flops 58662912 | bytes 7151616 | tf_op jit(solution)/shard_map/concatenate | solution.py:505
  280.8 8.6 %shard_map.280 = bf16[2,512,1792]{2,1,0:T(8,128)(2,1)} custom-call(s32[2,512,1]{2,1,0:T(8,128)} %get-tuple-element.170.src_ref, bf16[528,1024]{1,0:T(8,128)(2,1)} %fusion.56.left_ref, bf16[528,3584]{1,0:T(8,128)(2,1)} %fusion.22.right_ref), custom_call_target="tpu_custom_call" | custom-call | flops 1937768448 | bytes 8536064 | tf_op jit(solution)/shard_map/pallas_call | solution.py:114
  297.2 6.5 %collective-permute-done.24 = bf16[32,4096]{1,0:T(8,128)(2,1)S(1)} collective-permute-done((bf16[32,4096]{1,0:T(8,128)(2,1)S(1)}, bf16[32,4096]{1,0:T(8,128)(2,1)S(1)}, u32[]{:S(2)}, u32[]{:S(2)}) %collective-permute-start.24) | collective-permute-done | bytes 262176 | tf_op jit(solution)/shard_map/ppermute | solution.py:54
  303.7 7.5 %collective-permute-done.25 = bf16[32,4096]{1,0:T(8,128)(2,1)S(1)} collective-permute-done((bf16[32,4096]{1,0:T(8,128)(2,1)S(1)}, bf16[32,4096]{1,0:T(8,128)(2,1)S(1)}, u32[]{:S(2)}, u32[]{:S(2)}) %collective-permute-start.25) | collective-permute-done | bytes 262176 | tf_op jit(solution)/shard_map/ppermute | solution.py:54
  311.2 7.4 %collective-permute-done.26 = bf16[32,4096]{1,0:T(8,128)(2,1)S(1)} collective-permute-done((bf16[32,4096]{1,0:T(8,128)(2,1)S(1)}, bf16[32,4096]{1,0:T(8,128)(2,1)S(1)}, u32[]{:S(2)}, u32[]{:S(2)}) %collective-permute-start.26) | collective-permute-done | bytes 262176 | tf_op jit(solution)/shard_map/ppermute | solution.py:54
  323.3 12.1 %collective-permute-done.14 = bf16[256,1152]{1,0:T(8,128)(2,1)S(1)} collective-permute-done((bf16[256,1152]{1,0:T(8,128)(2,1)S(1)}, bf16[256,1152]{1,0:T(8,128)(2,1)S(1)}, u32[]{:S(2)}, u32[]{:S(2)}) %collective-permute-start.14) | collective-permute-done | bytes 589856 | tf_op jit(solution)/shard_map/ppermute | solution.py:54
  339.3 10.7 %shard_map.281 = (bf16[256,1792]{1,0:T(8,128)(2,1)}, bf16[256,1792]{1,0:T(8,128)(2,1)}, bf16[256,1792]{1,0:T(8,128)(2,1)}, bf16[256,1792]{1,0:T(8,128)(2,1)}) custom-call(s32[2,512,1]{2,1,0:T(8,128)} %get-tuple-element.171.src_ref, bf16[528,1024]{1,0:T(8,128)(2,1)} %fusion.56.left_ref, bf16[528,3584]{1,0:T(8,128)(2,1)} %fusion.22.right_ref, ...), custom_call_target="tpu_custom_call" | custom-call | flops 1937768448 | bytes 8536064 | tf_op jit(solution)/shard_map/pallas_call | solution.py:114
  352.7 18.0 %collective-permute-done.7 = bf16[256,1792]{1,0:T(8,128)(2,1)S(1)} collective-permute-done((bf16[256,1792]{1,0:T(8,128)(2,1)}, bf16[256,1792]{1,0:T(8,128)(2,1)S(1)}, u32[]{:S(2)}, u32[]{:S(2)}) %collective-permute-start.7) | collective-permute-done | bytes 917536 | tf_op jit(solution)/shard_map/ppermute | solution.py:54
  378.7 4.0 collective-permute-done.8
  386.5 13.1 %collective-permute-done.19 = bf16[32,2304]{1,0:T(8,128)(2,1)S(1)} collective-permute-done((bf16[32,2304]{1,0:T(8,128)(2,1)S(1)}, bf16[32,2304]{1,0:T(8,128)(2,1)S(1)}, u32[]{:S(2)}, u32[]{:S(2)}) %collective-permute-start.19) | collective-permute-done | bytes 147488 | tf_op jit(solution)/shard_map/ppermute | solution.py:54
  402.8 5.3 %collective-permute-done.12 = bf16[32,3584]{1,0:T(8,128)(2,1)S(1)} collective-permute-done((bf16[32,3584]{1,0:T(8,128)(2,1)S(1)}, bf16[32,3584]{1,0:T(8,128)(2,1)S(1)}, u32[]{:S(2)}, u32[]{:S(2)}) %collective-permute-start.12) | collective-permute-done | bytes 229408 | tf_op jit(solution)/shard_map/ppermute | solution.py:54
  (321 shorter events, 162.9 us)
Async XLA Ops:
  6.0 35.4 %collective-permute-start.1 = (bf16[512,448]{0,1:T(8,128)(2,1)}, bf16[512,448]{0,1:T(8,128)(2,1)}, u32[]{:S(2)}, u32[]{:S(2)}) collective-permute-start(bf16[512,448]{0,1:T(8,128)(2,1)} %convolution_convert_fusion.2), channel_id=1, source_target_pairs={{0,2},{2,4},{4,6},{6,8},{8,10},{10,12},{12,14},{14,16},{16,18},{18... | collective-permute-start | bytes 1376264 | tf_op jit(solution)/shard_map/ppermute | solution.py:38
  17.4 27.8 %collective-permute-start = (bf16[512,448]{0,1:T(8,128)(2,1)}, bf16[512,448]{0,1:T(8,128)(2,1)}, u32[]{:S(2)}, u32[]{:S(2)}) collective-permute-start(bf16[512,448]{0,1:T(8,128)(2,1)} %bitcast.6), channel_id=1, source_target_pairs={{0,2},{2,4},{4,6},{6,8},{8,10},{10,12},{12,14},{14,16},{16,18},{18... | collective-permute-start | bytes 1376264 | tf_op jit(solution)/shard_map/ppermute | solution.py:38
  79.4 38.8 %collective-permute-start.2 = (bf16[2,2048,512]{2,1,0:T(8,128)(2,1)}, bf16[2,2048,512]{2,1,0:T(8,128)(2,1)}, u32[]{:S(2)}, u32[]{:S(2)}) collective-permute-start(bf16[2,2048,512]{2,1,0:T(8,128)(2,1)} %shard_map.274), channel_id=1, source_target_pairs={{0,2},{1,3},{2,0},{3,1},{4,6},{5,7},{6,4},{7,5},{8,10},{9,11},{10,... | collective-permute-start | bytes 12582920 | tf_op jit(solution)/shard_map/ppermute | solution.py:54
  99.0 31.5 %collective-permute-start.3 = (bf16[2,512,2048]{2,1,0:T(8,128)(2,1)}, bf16[2,512,2048]{2,1,0:T(8,128)(2,1)}, u32[]{:S(2)}, u32[]{:S(2)}) collective-permute-start(bf16[2,512,2048]{2,1,0:T(8,128)(2,1)} %shard_map.275), channel_id=1, source_target_pairs={{0,2},{1,3},{2,0},{3,1},{4,6},{5,7},{6,4},{7,5},{8,10},{9,11},{10,... | collective-permute-start | bytes 12582920 | tf_op jit(solution)/shard_map/ppermute | solution.py:54
  127.5 39.4 %collective-permute-start.27 = (bf16[1024,512]{1,0:T(8,128)(2,1)}, bf16[1024,512]{1,0:T(8,128)(2,1)}, u32[]{:S(2)}, u32[]{:S(2)}) collective-permute-start(bf16[1024,512]{1,0:T(8,128)(2,1)} %get-tuple-element.37), channel_id=1, source_target_pairs={{0,1},{1,0},{2,3},{3,2},{4,5},{5,4},{6,7},{7,6},{8,9},{9,8},{10,11... | collective-permute-start | bytes 3145736 | tf_op jit(solution)/shard_map/ppermute | solution.py:54
  129.0 41.1 %collective-permute-start.28 = (bf16[1024,512]{1,0:T(8,128)(2,1)}, bf16[1024,512]{1,0:T(8,128)(2,1)}, u32[]{:S(2)}, u32[]{:S(2)}) collective-permute-start(bf16[1024,512]{1,0:T(8,128)(2,1)} %get-tuple-element.39), channel_id=1, source_target_pairs={{0,4},{1,5},{2,6},{3,7},{4,0},{5,1},{6,2},{7,3},{8,12},{9,13},{10,... | collective-permute-start | bytes 3145736 | tf_op jit(solution)/shard_map/ppermute | solution.py:54
  140.4 35.8 %collective-permute-start.20 = (bf16[256,2048]{1,0:T(8,128)(2,1)}, bf16[256,2048]{1,0:T(8,128)(2,1)}, u32[]{:S(2)}, u32[]{:S(2)}) collective-permute-start(bf16[256,2048]{1,0:T(8,128)(2,1)} %get-tuple-element.42), channel_id=1, source_target_pairs={{0,1},{1,0},{2,3},{3,2},{4,5},{5,4},{6,7},{7,6},{8,9},{9,8},{10,11... | collective-permute-start | bytes 3145736 | tf_op jit(solution)/shard_map/ppermute | solution.py:54
  140.9 39.3 %collective-permute-start.21 = (bf16[256,2048]{1,0:T(8,128)(2,1)}, bf16[256,2048]{1,0:T(8,128)(2,1)}, u32[]{:S(2)}, u32[]{:S(2)}) collective-permute-start(bf16[256,2048]{1,0:T(8,128)(2,1)} %get-tuple-element.44), channel_id=1, source_target_pairs={{0,4},{1,5},{2,6},{3,7},{4,0},{5,1},{6,2},{7,3},{8,12},{9,13},{10,... | collective-permute-start | bytes 3145736 | tf_op jit(solution)/shard_map/ppermute | solution.py:54
  159.1 43.2 %collective-permute-start.4 = (bf16[2,512,1152]{2,1,0:T(8,128)(2,1)}, bf16[2,512,1152]{2,1,0:T(8,128)(2,1)S(1)}, u32[]{:S(2)}, u32[]{:S(2)}) collective-permute-start(bf16[2,512,1152]{2,1,0:T(8,128)(2,1)} %shard_map.278), channel_id=1, source_target_pairs={{0,2},{1,3},{2,0},{3,1},{4,6},{5,7},{6,4},{7,5},{8,10},{9,11},{10,... | collective-permute-start | bytes 7077896 | tf_op jit(solution)/shard_map/ppermute | solution.py:54
  168.5 20.5 %collective-permute-start.29 = (bf16[512,512]{1,0:T(8,128)(2,1)S(1)}, bf16[512,512]{1,0:T(8,128)(2,1)S(1)}, u32[]{:S(2)}, u32[]{:S(2)}) collective-permute-start(bf16[512,512]{1,0:T(8,128)(2,1)S(1)} %get-tuple-element.132), channel_id=1, source_target_pairs={{0,4},{1,5},{2,6},{3,7},{4,0},{5,1},{6,2},{7,3},{8,12},{9,13},{10,... | collective-permute-start | bytes 1572872 | tf_op jit(solution)/shard_map/ppermute | solution.py:54
  171.6 17.5 %collective-permute-start.30 = (bf16[512,512]{1,0:T(8,128)(2,1)S(1)}, bf16[512,512]{1,0:T(8,128)(2,1)S(1)}, u32[]{:S(2)}, u32[]{:S(2)}) collective-permute-start(bf16[512,512]{1,0:T(8,128)(2,1)S(1)} %get-tuple-element.134), channel_id=1, source_target_pairs={{0,1},{1,0},{2,3},{3,2},{4,5},{5,4},{6,7},{7,6},{8,9},{9,8},{10,11... | collective-permute-start | bytes 1572872 | tf_op jit(solution)/shard_map/ppermute | solution.py:54
  178.6 20.3 %collective-permute-start.22 = (bf16[128,2048]{1,0:T(8,128)(2,1)S(1)}, bf16[128,2048]{1,0:T(8,128)(2,1)S(1)}, u32[]{:S(2)}, u32[]{:S(2)}) collective-permute-start(bf16[128,2048]{1,0:T(8,128)(2,1)S(1)} %get-tuple-element.139), channel_id=1, source_target_pairs={{0,4},{1,5},{2,6},{3,7},{4,0},{5,1},{6,2},{7,3},{8,12},{9,13},{10,... | collective-permute-start | bytes 1572872 | tf_op jit(solution)/shard_map/ppermute | solution.py:54
  182.6 18.8 %collective-permute-start.23 = (bf16[128,2048]{1,0:T(8,128)(2,1)S(1)}, bf16[128,2048]{1,0:T(8,128)(2,1)S(1)}, u32[]{:S(2)}, u32[]{:S(2)}) collective-permute-start(bf16[128,2048]{1,0:T(8,128)(2,1)S(1)} %get-tuple-element.141), channel_id=1, source_target_pairs={{0,1},{1,0},{2,3},{3,2},{4,5},{5,4},{6,7},{7,6},{8,9},{9,8},{10,11... | collective-permute-start | bytes 1572872 | tf_op jit(solution)/shard_map/ppermute | solution.py:54
  190.3 103.1 %collective-permute-start.31 = (bf16[128,1024]{1,0:T(8,128)(2,1)}, bf16[128,1024]{1,0:T(8,128)(2,1)}, u32[]{:S(2)}, u32[]{:S(2)}) collective-permute-start(bf16[128,1024]{1,0:T(8,128)(2,1)} %get-tuple-element.128), channel_id=1, source_target_pairs={{0,8},{1,9},{2,10},{3,11},{4,12},{5,13},{6,14},{7,15},{8,0},{9,1},... | collective-permute-start | bytes 786440 | tf_op jit(solution)/shard_map/ppermute | solution.py:54
  191.6 101.8 %collective-permute-start.32 = (bf16[128,1024]{1,0:T(8,128)(2,1)}, bf16[128,1024]{1,0:T(8,128)(2,1)}, u32[]{:S(2)}, u32[]{:S(2)}) collective-permute-start(bf16[128,1024]{1,0:T(8,128)(2,1)} %get-tuple-element.130), channel_id=1, source_target_pairs={{0,16},{1,17},{2,18},{3,19},{4,20},{5,21},{6,22},{7,23},{8,24},{9,... | collective-permute-start | bytes 786440 | tf_op jit(solution)/shard_map/ppermute | solution.py:54
  199.0 96.1 %collective-permute-start.33 = (bf16[128,1024]{1,0:T(8,128)(2,1)}, bf16[128,1024]{1,0:T(8,128)(2,1)}, u32[]{:S(2)}, u32[]{:S(2)}) collective-permute-start(bf16[128,1024]{1,0:T(8,128)(2,1)} %get-tuple-element.129), channel_id=1, source_target_pairs={{0,24},{1,25},{2,26},{3,27},{4,28},{5,29},{6,30},{7,31},{8,16},{9,... | collective-permute-start | bytes 786440 | tf_op jit(solution)/shard_map/ppermute | solution.py:54
  289.4 48.0 %collective-permute-start.5 = (bf16[2,512,1792]{2,1,0:T(8,128)(2,1)}, bf16[2,512,1792]{2,1,0:T(8,128)(2,1)S(1)}, u32[]{:S(2)}, u32[]{:S(2)}) collective-permute-start(bf16[2,512,1792]{2,1,0:T(8,128)(2,1)} %shard_map.280), channel_id=1, source_target_pairs={{0,2},{1,3},{2,0},{3,1},{4,6},{5,7},{6,4},{7,5},{8,10},{9,11},{10,... | collective-permute-start | bytes 11010056 | tf_op jit(solution)/shard_map/ppermute | solution.py:54
  290.9 12.8 %collective-permute-start.24 = (bf16[32,4096]{1,0:T(8,128)(2,1)S(1)}, bf16[32,4096]{1,0:T(8,128)(2,1)S(1)}, u32[]{:S(2)}, u32[]{:S(2)}) collective-permute-start(bf16[32,4096]{1,0:T(8,128)(2,1)S(1)} %get-tuple-element.135), channel_id=1, source_target_pairs={{0,8},{1,9},{2,10},{3,11},{4,12},{5,13},{6,14},{7,15},{8,0},{9,1},... | collective-permute-start | bytes 786440 | tf_op jit(solution)/shard_map/ppermute | solution.py:54
  293.5 17.8 %collective-permute-start.25 = (bf16[32,4096]{1,0:T(8,128)(2,1)S(1)}, bf16[32,4096]{1,0:T(8,128)(2,1)S(1)}, u32[]{:S(2)}, u32[]{:S(2)}) collective-permute-start(bf16[32,4096]{1,0:T(8,128)(2,1)S(1)} %get-tuple-element.137), channel_id=1, source_target_pairs={{0,16},{1,17},{2,18},{3,19},{4,20},{5,21},{6,22},{7,23},{8,24},{9,... | collective-permute-start | bytes 786440 | tf_op jit(solution)/shard_map/ppermute | solution.py:54
  293.5 25.1 %collective-permute-start.26 = (bf16[32,4096]{1,0:T(8,128)(2,1)S(1)}, bf16[32,4096]{1,0:T(8,128)(2,1)S(1)}, u32[]{:S(2)}, u32[]{:S(2)}) collective-permute-start(bf16[32,4096]{1,0:T(8,128)(2,1)S(1)} %get-tuple-element.136), channel_id=1, source_target_pairs={{0,24},{1,25},{2,26},{3,27},{4,28},{5,29},{6,30},{7,31},{8,16},{9,... | collective-permute-start | bytes 786440 | tf_op jit(solution)/shard_map/ppermute | solution.py:54
  320.5 14.9 %collective-permute-start.14 = (bf16[256,1152]{1,0:T(8,128)(2,1)S(1)}, bf16[256,1152]{1,0:T(8,128)(2,1)S(1)}, u32[]{:S(2)}, u32[]{:S(2)}) collective-permute-start(bf16[256,1152]{1,0:T(8,128)(2,1)S(1)} %copy-done.61), channel_id=1, source_target_pairs={{0,4},{1,5},{2,6},{3,7},{4,0},{5,1},{6,2},{7,3},{8,12},{9,13},{10,... | collective-permute-start | bytes 1769480 | tf_op jit(solution)/shard_map/ppermute | solution.py:54
  321.2 15.0 %collective-permute-start.13 = (bf16[256,1152]{1,0:T(8,128)(2,1)S(1)}, bf16[256,1152]{1,0:T(8,128)(2,1)S(1)}, u32[]{:S(2)}, u32[]{:S(2)}) collective-permute-start(bf16[256,1152]{1,0:T(8,128)(2,1)S(1)} %copy-done.60), channel_id=1, source_target_pairs={{0,1},{1,0},{2,3},{3,2},{4,5},{5,4},{6,7},{7,6},{8,9},{9,8},{10,11... | collective-permute-start | bytes 1769480 | tf_op jit(solution)/shard_map/ppermute | solution.py:54
  335.6 17.0 %collective-permute-start.16 = (bf16[128,1152]{1,0:T(8,128)(2,1)S(1)}, bf16[128,1152]{1,0:T(8,128)(2,1)S(1)}, u32[]{:S(2)}, u32[]{:S(2)}) collective-permute-start(bf16[128,1152]{1,0:T(8,128)(2,1)S(1)} %get-tuple-element.155), channel_id=1, source_target_pairs={{0,1},{1,0},{2,3},{3,2},{4,5},{5,4},{6,7},{7,6},{8,9},{9,8},{10,11... | collective-permute-start | bytes 884744 | tf_op jit(solution)/shard_map/ppermute | solution.py:54
  336.3 16.2 %collective-permute-start.15 = (bf16[128,1152]{1,0:T(8,128)(2,1)S(1)}, bf16[128,1152]{1,0:T(8,128)(2,1)S(1)}, u32[]{:S(2)}, u32[]{:S(2)}) collective-permute-start(bf16[128,1152]{1,0:T(8,128)(2,1)S(1)} %get-tuple-element.153), channel_id=1, source_target_pairs={{0,4},{1,5},{2,6},{3,7},{4,0},{5,1},{6,2},{7,3},{8,12},{9,13},{10,... | collective-permute-start | bytes 884744 | tf_op jit(solution)/shard_map/ppermute | solution.py:54
  350.0 20.7 %collective-permute-start.7 = (bf16[256,1792]{1,0:T(8,128)(2,1)}, bf16[256,1792]{1,0:T(8,128)(2,1)S(1)}, u32[]{:S(2)}, u32[]{:S(2)}) collective-permute-start(bf16[256,1792]{1,0:T(8,128)(2,1)} %get-tuple-element.57), channel_id=1, source_target_pairs={{0,4},{1,5},{2,6},{3,7},{4,0},{5,1},{6,2},{7,3},{8,12},{9,13},{10,... | collective-permute-start | bytes 2752520 | tf_op jit(solution)/shard_map/ppermute | solution.py:54
  351.0 21.9 %collective-permute-start.6 = (bf16[256,1792]{1,0:T(8,128)(2,1)}, bf16[256,1792]{1,0:T(8,128)(2,1)S(1)}, u32[]{:S(2)}, u32[]{:S(2)}) collective-permute-start(bf16[256,1792]{1,0:T(8,128)(2,1)} %get-tuple-element.55), channel_id=1, source_target_pairs={{0,1},{1,0},{2,3},{3,2},{4,5},{5,4},{6,7},{7,6},{8,9},{9,8},{10,11... | collective-permute-start | bytes 2752520 | tf_op jit(solution)/shard_map/ppermute | solution.py:54
  372.1 10.7 %collective-permute-start.9 = (bf16[128,1792]{1,0:T(8,128)(2,1)S(1)}, bf16[128,1792]{1,0:T(8,128)(2,1)S(1)}, u32[]{:S(2)}, u32[]{:S(2)}) collective-permute-start(bf16[128,1792]{1,0:T(8,128)(2,1)S(1)} %get-tuple-element.148), channel_id=1, source_target_pairs={{0,1},{1,0},{2,3},{3,2},{4,5},{5,4},{6,7},{7,6},{8,9},{9,8},{10,11... | collective-permute-start | bytes 1376264 | tf_op jit(solution)/shard_map/ppermute | solution.py:54
  375.2 11.3 %collective-permute-start.18 = (bf16[32,2304]{1,0:T(8,128)(2,1)S(1)}, bf16[32,2304]{1,0:T(8,128)(2,1)S(1)}, u32[]{:S(2)}, u32[]{:S(2)}) collective-permute-start(bf16[32,2304]{1,0:T(8,128)(2,1)S(1)} %get-tuple-element.151), channel_id=1, source_target_pairs={{0,16},{1,17},{2,18},{3,19},{4,20},{5,21},{6,22},{7,23},{8,24},{9,... | collective-permute-start | bytes 442376 | tf_op jit(solution)/shard_map/ppermute | solution.py:54
  377.1 22.5 %collective-permute-start.19 = (bf16[32,2304]{1,0:T(8,128)(2,1)S(1)}, bf16[32,2304]{1,0:T(8,128)(2,1)S(1)}, u32[]{:S(2)}, u32[]{:S(2)}) collective-permute-start(bf16[32,2304]{1,0:T(8,128)(2,1)S(1)} %get-tuple-element.150), channel_id=1, source_target_pairs={{0,24},{1,25},{2,26},{3,27},{4,28},{5,29},{6,30},{7,31},{8,16},{9,... | collective-permute-start | bytes 442376 | tf_op jit(solution)/shard_map/ppermute | solution.py:54
  383.0 17.5 %collective-permute-start.10 = (bf16[32,3584]{1,0:T(8,128)(2,1)S(1)}, bf16[32,3584]{1,0:T(8,128)(2,1)S(1)}, u32[]{:S(2)}, u32[]{:S(2)}) collective-permute-start(bf16[32,3584]{1,0:T(8,128)(2,1)S(1)} %get-tuple-element.142), channel_id=1, source_target_pairs={{0,8},{1,9},{2,10},{3,11},{4,12},{5,13},{6,14},{7,15},{8,0},{9,1},... | collective-permute-start | bytes 688136 | tf_op jit(solution)/shard_map/ppermute | solution.py:54
  383.0 19.8 %collective-permute-start.11 = (bf16[32,3584]{1,0:T(8,128)(2,1)S(1)}, bf16[32,3584]{1,0:T(8,128)(2,1)S(1)}, u32[]{:S(2)}, u32[]{:S(2)}) collective-permute-start(bf16[32,3584]{1,0:T(8,128)(2,1)S(1)} %get-tuple-element.144), channel_id=1, source_target_pairs={{0,16},{1,17},{2,18},{3,19},{4,20},{5,21},{6,22},{7,23},{8,24},{9,... | collective-permute-start | bytes 688136 | tf_op jit(solution)/shard_map/ppermute | solution.py:54
  385.0 23.1 %collective-permute-start.12 = (bf16[32,3584]{1,0:T(8,128)(2,1)S(1)}, bf16[32,3584]{1,0:T(8,128)(2,1)S(1)}, u32[]{:S(2)}, u32[]{:S(2)}) collective-permute-start(bf16[32,3584]{1,0:T(8,128)(2,1)S(1)} %get-tuple-element.143), channel_id=1, source_target_pairs={{0,24},{1,25},{2,26},{3,27},{4,28},{5,29},{6,30},{7,31},{8,16},{9,... | collective-permute-start | bytes 688136 | tf_op jit(solution)/shard_map/ppermute | solution.py:54
  (68 other events, 628.8 us)
